TPU v7x, 512 devices: a whole 4x8x8 slice. The times are simulated.
512 devices in a mesh: vol: 64 (over z, x, y_hi), path: 8 (over y_lo, core).
Axes of the slice: x: 4, y: 8 (y_hi: 2, y_lo: 4; y = y_hi * 4 + y_lo), z: 8, core: 2. Of those that a mesh axis runs over, the one named last changes fastest.
Arguments:
- factors: bfloat16 [16, 8192], P(None, 'path'), may hold values from -6 to 6
- payoff: float32 [4, 8192], P(None, 'path'), may hold values from -6 to 6
- terminal: float32 [64, 8192], P('vol', 'path'), may hold values from 0.5 to 4
- decisions: int32 [3, 64, 8192], P(None, 'vol', 'path'), may hold values 0 or 1
- level_range: int32 [4, 2], replicated, may hold values from 1 to 63, as said below
- w_in_master: float32 [64, 16, 1024], P('vol'), may hold values from -1.5 to 1.5
- w_mid_master: float32 [64, 1024, 1024], P('vol', 'path'), may hold values from -0.1875 to 0.1875
- vec_master: float32 [64, 3, 1024], P('vol'), may hold values from -0.6 to 0.6
- w_in_copy: bfloat16 [64, 16, 1024], P('vol'), may hold values from -1.5 to 1.5
- w_mid_copy: bfloat16 [64, 1024, 1024], P('vol', 'path'), may hold values from -0.1875 to 0.1875
- mom_in: float32 [64, 16, 1024], P('vol'), may hold values from -0.6 to 0.6
- mom_mid: float32 [64, 1024, 1024], P('vol', 'path'), may hold values from -0.6 to 0.6
- mom_vec: float32 [64, 3, 1024], P('vol'), may hold values from -0.6 to 0.6
Outputs:
- level_value: float32 [64], P('vol')
- new_w_in: float32 [64, 16, 1024], P('vol')
- new_w_mid: float32 [64, 1024, 1024], P('vol', 'path')
- new_vec: float32 [64, 3, 1024], P('vol')
- new_mom_in: float32 [64, 16, 1024], P('vol')
- new_mom_mid: float32 [64, 1024, 1024], P('vol', 'path')
- new_mom_vec: float32 [64, 3, 1024], P('vol')
- new_in_copy: bfloat16 [64, 16, 1024], P('vol')
- new_mid_copy: bfloat16 [64, 1024, 1024], P('vol', 'path')
Inputs may be any that keep to these rules, and one draw needn't show every extreme that they name: At every date level_range[s, 0] <= level_range[s, 1] and level 0 lies below the range; at dates 1 to 3 the range starts at level 1; at date 0 the range holds exactly 32 levels.
All inputs are finite; a program needn't handle non-finite values. No bound on the sum of `decisions` on one device may be relied on, other than what follows from the above.
Results may differ from a plain program's by a relative error of at most 0.015.
Values may be sent and summed in bfloat16 or wider, within the bound.
A program may use at most 64 MiB of HBM per device.

v0:
```python
import jax
import jax.numpy as jnp
from jax import lax
from jax.sharding import PartitionSpec as P

MOMENTUM = 0.9
STEP_SIZE = 0.01


def from_behind(value, axis, steps):
    count = lax.axis_size(axis)
    leading, last = (max(0, -steps), min(count, count - steps))
    return lax.ppermute(value, axis, [(source, source + steps) for source in range(leading, last)])


def copy_for_each(value, axis):
    length = lax.axis_size(axis)
    return lax.all_to_all(
        jnp.broadcast_to(value[None], (length, *value.shape)), axis, 0, 0, tiled=True
    )


def of_everyone(value, axis):
    everything = copy_for_each(value, axis)
    return jnp.sum(everything, axis=0)


def together(arrays, axis):
    line, at, outs = (jnp.concatenate([a.reshape(-1) for a in arrays]), 0, [])
    so_far = of_everyone(line, axis)
    for a in arrays:
        outs.append(so_far[at : at + a.size].reshape(a.shape))
        at += a.size
    return tuple(outs)


def silu_parts(preact):
    squash = jax.nn.sigmoid(preact)
    return (preact * squash, squash * (1.0 + preact * (1.0 - squash)))


def network_pass(w_first, w_second, vectors, features, gain_row, enabled):
    pre_one = (
        lax.dot_general(
            features, w_first, (((0,), (0,)), ((), ())), preferred_element_type=jnp.float32
        )
        + vectors[0]
    )
    act_one, slope_one = silu_parts(pre_one)
    hidden_one = act_one.astype(jnp.bfloat16)
    pre_two = jnp.dot(hidden_one, w_second, preferred_element_type=jnp.float32) + vectors[1]
    act_two, slope_two = silu_parts(pre_two)
    hidden_two = act_two.astype(jnp.bfloat16)
    logits = jnp.sum(hidden_two.astype(jnp.float32) * vectors[2], axis=1)
    chance = jax.nn.sigmoid(logits)
    d_logit = jnp.where(enabled, -gain_row * chance * (1.0 - chance), 0.0)
    d_head = jnp.sum(d_logit[:, None] * hidden_two.astype(jnp.float32), axis=0)
    d_pre_two = d_logit[:, None] * vectors[2] * slope_two
    d_bias_two = jnp.sum(d_pre_two, axis=0)
    d_two_low = d_pre_two.astype(jnp.bfloat16)
    d_hidden_one = lax.dot_general(
        d_two_low, w_second, (((1,), (1,)), ((), ())), preferred_element_type=jnp.float32
    )
    d_pre_one = d_hidden_one * slope_one
    d_bias_one = jnp.sum(d_pre_one, axis=0)
    d_first = jnp.dot(features, d_pre_one.astype(jnp.bfloat16), preferred_element_type=jnp.float32)
    d_vectors = jnp.stack([d_bias_one, d_bias_two, d_head])
    value_sum = jnp.where(enabled, jnp.sum(chance * gain_row), 0.0)
    return (hidden_one, d_two_low, d_first, d_vectors, value_sum)


def row_product(hidden_one, d_two_low):
    return lax.dot_general(
        hidden_one, d_two_low, (((0,), (0,)), ((), ())), preferred_element_type=jnp.float32
    )


def lower_neighbour(values):
    return from_behind(values, "vol", 1)


def full_rows(row_shard):
    return lax.all_gather(row_shard, "path", axis=0, tiled=True)


def shards(
    factors,
    payoff,
    terminal,
    decisions,
    level_range,
    w_in_master,
    w_mid_master,
    vec_master,
    w_in_copy,
    w_mid_copy,
    mom_in,
    mom_mid,
    mom_vec,
):
    level_here = lax.axis_index("vol")
    dates = payoff.shape[0]
    paths_here = payoff.shape[1]
    carry_value = terminal[0]
    for date_index in range(dates - 1, 0, -1):
        lower_row = lower_neighbour(carry_value)
        lower_end = level_range[date_index, 0]
        upper_end = level_range[date_index, 1]
        inside = jnp.logical_and(level_here >= lower_end, level_here <= upper_end)
        taken_now = jnp.where(
            level_here > upper_end,
            1.0,
            jnp.where(inside, decisions[date_index - 1, 0].astype(jnp.float32), 0.0),
        )
        carry_value = taken_now * (payoff[date_index] + lower_row) + (1.0 - taken_now) * carry_value
    lower_row = lower_neighbour(carry_value)
    gain_row = payoff[0] + lower_row - carry_value
    low_now = level_range[0, 0]
    high_now = level_range[0, 1]
    active = jnp.logical_and(level_here >= low_now, level_here <= high_now)
    forced = jnp.where(level_here > high_now, 1.0, 0.0)
    first_copy = w_in_copy[0]
    vectors = vec_master[0]
    second_full = full_rows(w_mid_copy[0])
    hidden_one, d_two_low, d_first, d_vectors, value_sum = network_pass(
        first_copy, second_full, vectors, factors, gain_row, active
    )
    mid_grad = lax.psum_scatter(
        row_product(hidden_one, d_two_low).astype(jnp.bfloat16),
        "path",
        scatter_dimension=0,
        tiled=True,
    ).astype(jnp.float32)
    value_local = jnp.where(active, value_sum, forced * jnp.sum(gain_row)) + jnp.sum(carry_value)
    d_first, d_vectors, value_local = together((d_first, d_vectors, value_local), "path")
    paths_total = paths_here * lax.axis_size("path")
    level_value = (value_local / paths_total)[None]
    new_mom_in = MOMENTUM * mom_in + d_first[None]
    new_mom_mid = MOMENTUM * mom_mid + mid_grad[None]
    new_mom_vec = MOMENTUM * mom_vec + d_vectors[None]
    new_w_in = w_in_master - STEP_SIZE * new_mom_in
    new_w_mid = w_mid_master - STEP_SIZE * new_mom_mid
    new_vec = vec_master - STEP_SIZE * new_mom_vec
    return (
        level_value,
        new_w_in,
        new_w_mid,
        new_vec,
        new_mom_in,
        new_mom_mid,
        new_mom_vec,
        new_w_in.astype(jnp.bfloat16),
        new_w_mid.astype(jnp.bfloat16),
    )


def solution(mesh):
    in_specs = (
        P(None, "path"),
        P(None, "path"),
        P("vol", "path"),
        P(None, "vol", "path"),
        P(),
        P("vol", None, None),
        P("vol", "path", None),
        P("vol", None, None),
        P("vol", None, None),
        P("vol", "path", None),
        P("vol", None, None),
        P("vol", "path", None),
        P("vol", None, None),
    )
    out_specs = (
        P("vol"),
        P("vol", None, None),
        P("vol", "path", None),
        P("vol", None, None),
        P("vol", None, None),
        P("vol", "path", None),
        P("vol", None, None),
        P("vol", None, None),
        P("vol", "path", None),
    )
    return jax.shard_map(shards, mesh=mesh, in_specs=in_specs, out_specs=out_specs, check_vma=False)
```

profile of v0, /device:TPU:1, one launch (start us, length us, event | category | flops | bytes accessed | tf_op | source)
XLA Modules:
  0.0 135.9 jit_solution(5936669052276414330)
XLA Ops:
  7.2 0.0 copy-start
  7.2 0.0 all-gather.3.cloned.1.call-start
  7.2 0.7 all-gather.3.cloned.1.call-update
  7.9 0.0 reduce-scatter.2.cloned.1.call-start
  8.0 8.3 %collective-permute-start = (f32[1024]{0:T(1024)}, f32[1024]{0:T(1024)S(1)}, u32[]{:S(2)}, u32[]{:S(2)}) collective-permute-start(f32[1024]{0:T(1024)} %bitcast.66), channel_id=1, source_target_pairs={{0,8},{8,16},{16,24},{24,32},{32,40},{40,48},{48,56},{56,64},{64,7... | collective-permute-start | bytes 12296 | tf_op jit(solution)/shard_map/ppermute | solution.py:13
  16.3 1.6 %fusion.21 = (s32[1,1]{0,1:T(1,128)}, s32[1,1]{0,1:T(1,128)}, s32[1,1]{0,1:T(1,128)}, s32[1,1]{0,1:T(1,128)}, s32[1,1]{0,1:T(1,128)}, /*index=5*/s32[1,1]{0,1:T(1,128)}, s32[1,1]{0,1:T(1,128)}, s32[1,1]{0,1:T(1,128)}) fusion(s32[4,2]{0,1:T(2,128)} %param.17), kind=kLoop, calls=%fused_computation.49 | loop fusion | bytes 64 | tf_op jit(solution)/shard_map/slice | solution.py:107
  23.7 0.9 fusion.19
  24.6 0.7 broadcast_select_fusion.5
  25.3 0.7 multiply_add_fusion.4
  26.0 2.7 %collective-permute-start.1 = (f32[1024]{0:T(1024)S(1)}, f32[1024]{0:T(1024)S(1)}, u32[]{:S(2)}, u32[]{:S(2)}) collective-permute-start(f32[1024]{0:T(1024)S(1)} %multiply_add_fusion.4), channel_id=1, source_target_pairs={{0,8},{8,16},{16,24},{24,32},{32,40},{40,48},{48,56},{56,64},{64,7... | collective-permute-start | bytes 12296 | tf_op jit(solution)/shard_map/ppermute | solution.py:13
  28.7 3.4 %fusion.12 = f32[1024,1024]{1,0:T(8,128)} fusion(bf16[16,1024]{1,0:T(8,128)(2,1)S(1)} %copy-done, bf16[1,16,1024]{2,1,0:T(8,128)(2,1)} %param.21), kind=kOutput, calls=%fused_computation.24 | convolution fusion | flops 33554432 | bytes 4259840 | tf_op jit(solution)/shard_map/dot_general | solution.py:44
  32.1 7.5 %collective-permute-start.2 = (f32[1024]{0:T(1024)S(1)}, f32[1024]{0:T(1024)S(1)}, u32[]{:S(2)}, u32[]{:S(2)}) collective-permute-start(f32[1024]{0:T(1024)S(1)} %multiply_add_fusion.3), channel_id=1, source_target_pairs={{0,8},{8,16},{16,24},{24,32},{32,40},{40,48},{48,56},{56,64},{64,7... | collective-permute-start | bytes 12296 | tf_op jit(solution)/shard_map/ppermute | solution.py:13
  41.6 0.6 fusion.18
  42.2 6.3 %collective-permute-start.3 = (f32[1024]{0:T(1024)S(1)}, f32[1024]{0:T(1024)S(1)}, u32[]{:S(2)}, u32[]{:S(2)}) collective-permute-start(f32[1024]{0:T(1024)S(1)} %get-tuple-element.24), channel_id=1, source_target_pairs={{0,8},{8,16},{16,24},{24,32},{32,40},{40,48},{48,56},{56,64},{64,7... | collective-permute-start | bytes 12296 | tf_op jit(solution)/shard_map/ppermute | solution.py:13
  48.5 7.5 %all-gather.3.cloned.1.call-done = bf16[1,1024,1024]{2,1,0:T(8,128)(2,1)} async-done(((bf16[1,128,1024]{2,1,0:T(8,128)(2,1)}), bf16[1,1024,1024]{2,1,0:T(8,128)(2,1)}) %all-gather.3.cloned.1.call-update) | async-done | bytes 2097168 | tf_op jit(solution)/shard_map/all_gather | solution.py:83
  55.9 5.9 %fusion = (f32[1024]{0:T(1024)S(1)}, bf16[1024,1024]{1,0:T(8,128)(2,1)S(1)}, f32[1024,1024]{1,0:T(8,128)S(1)}) fusion(f32[1024]{0:T(1024)S(1)} %bitcast.62, f32[1024]{0:T(1024)S(1)} %bitcast.58, bf16[1,1024,1024]{2,1,0:T(8,128)(2,1)} %all-gather.3.cloned.1.call-done, f32[1024,1024]{1,0:T(8,128)} %fusion.12, f32[1024]{0:T(1024)S(1)} %bitcast.69), kind=kOutput, calls=%fused_computation.2 | convolution fusion | flops 2163211264 | bytes 12599296 | tf_op jit(solution)/shard_map/dot_general | solution.py:51
  61.9 1.9 %copy-done.2 = f32[1024,1024]{1,0:T(8,128)} copy-done((f32[1024,1024]{1,0:T(8,128)}, f32[1024,1024]{1,0:T(8,128)S(1)}, u32[]{:S(2)}) %copy-start.2) | copy-done | bytes 4194328
  63.8 5.2 %convolution_convert_fusion = bf16[1024,1024]{1,0:T(8,128)(2,1)} fusion(f32[1024,1024]{1,0:T(8,128)S(1)} %copy-done.1, f32[1024]{0:T(1024)S(1)} %bitcast.70, f32[1024,1024]{1,0:T(8,128)S(1)} %get-tuple-element.45, f32[1024]{0:T(1024)S(1)} %get-tuple-element.21, f32[1024]{0:T(1024)S(1)} %bitcast.63, f32[1024]{0:T(1024)S(1)} %bitcast.59), kind=kOutput, calls=%fused_computation.15 | convolution fusion | flops 2166358016 | bytes 10502144 | tf_op jit(solution)/shard_map/dot_general | solution.py:73
  69.0 0.0 reduce-scatter.2.cloned.1.call-update
  69.1 4.0 %fusion.14 = (f32[1024]{0:T(1024)S(1)}, f32[1024]{0:T(1024)S(1)}) fusion(f32[1024,1024]{1,0:T(8,128)} %copy-done.2, f32[1024]{0:T(1024)S(1)} %bitcast.60, f32[1024]{0:T(1024)S(1)} %bitcast.64, f32[1024]{0:T(1024)S(1)} %get-tuple-element.21, bf16[1024,1024]{1,0:T(8,128)(2,1)S(1)} %get-tuple-element.26), kind=kLoop, calls=%fused_computation.42 | loop fusion | flops 14678016 | bytes 6311936 | tf_op jit(solution)/shard_map/reduce_sum | solution.py:59
  73.0 0.6 fusion.15
  74.3 7.2 %fusion.22 = (f32[1024]{0:T(1024)S(1)}, bf16[1024,1024]{1,0:T(8,128)(2,1)S(1)}) fusion(f32[1024,1024]{1,0:T(8,128)} %fusion.12, f32[1024]{0:T(1024)S(1)} %bitcast.71, bf16[1,1024,1024]{2,1,0:T(8,128)(2,1)} %all-gather.3.cloned.1.call-done, f32[1024,1024]{1,0:T(8,128)} %copy-done.2, f32[1024]{0:T(1024)S(1)} %bitcast.61, f32[1024]{0:T(1024)S(1)} %bitcast.65, ...), kind=kOutput, calls=%fused_computation.50 | convolution fusion | flops 2170551296 | bytes 12603392 | tf_op jit(solution)/shard_map/dot_general | solution.py:61
  81.5 0.0 copy-start.5
  81.6 0.4 fusion.7
  83.3 0.3 broadcast_in_dim.36
  83.7 33.0 %all_to_all.6 = f32[8,1,19457]{2,1,0:T(1,128)S(1)} all-to-all(f32[8,1,19457]{2,1,0:T(1,128)S(1)} %broadcast_in_dim.36), channel_id=1, replica_groups=mesh['vol'=64,'path'=8] {'path'}, dimensions={0} | all-to-all | bytes 1245248 | tf_op jit(solution)/shard_map/all_to_all | solution.py:18
  116.7 0.5 reduce_sum.79
  117.2 0.5 slice.88
  118.4 0.6 multiply_subtract_fusion.2
  119.0 0.7 fusion.17
  119.7 6.0 %reduce-scatter.2.cloned.1.call-done = bf16[128,1024]{1,0:T(8,128)(2,1)} async-done(((bf16[1024,1024]{1,0:T(8,128)(2,1)}), bf16[128,1024]{1,0:T(8,128)(2,1)}) %reduce-scatter.2.cloned.1.call-update) | async-done | bytes 262160 | tf_op jit(solution)/shard_map/reduce_scatter | solution.py:128
  125.7 2.1 %fusion.16 = (bf16[1,128,1024]{2,1,0:T(8,128)(2,1)}, f32[1,128,1024]{2,1,0:T(8,128)}, f32[1,128,1024]{2,1,0:T(8,128)}) fusion(f32[1,128,1024]{2,1,0:T(8,128)S(1)} %copy-done.3, bf16[128,1024]{1,0:T(8,128)(2,1)} %reduce-scatter.2.cloned.1.call-done, f32[1,128,1024]{2,1,0:T(8,128)S(1)} %copy-done.4), kind=kLoop, calls=%fused_computation.44 | loop fusion | flops 786432 | bytes 2621440 | tf_op jit(solution)/shard_map/convert_element_type | solution.py:153
  (29 shorter events, 0.2 us)
Async XLA Ops:
  7.2 21.5 %copy-start = (bf16[16,1024]{1,0:T(8,128)(2,1)S(1)}, bf16[16,1024]{1,0:T(8,128)(2,1)}, u32[]{:S(2)}) copy-start(bf16[16,1024]{1,0:T(8,128)(2,1)} %param.13) | copy-start | bytes 98308
  7.2 32.4 %copy-start.7 = (f32[1,3,1024]{2,0,1:T(1,128)S(1)}, f32[1,3,1024]{2,0,1:T(1,128)}, u32[]{:S(2)}) copy-start(f32[1,3,1024]{2,0,1:T(1,128)} %param.20) | copy-start | bytes 36868
  7.2 48.7 %all-gather.3.cloned.1.call-start = ((), (), s32[]{:S(2)}) async-start(), calls=%async_computation.3 | async-start | bytes 2359296 | tf_op jit(solution)/shard_map/all_gather | solution.py:83
  7.9 117.8 %reduce-scatter.2.cloned.1.call-start = ((), (), s32[]{:S(2)}) async-start(), calls=%async_computation.2 | async-start | bytes 2359296 | tf_op jit(solution)/shard_map/reduce_scatter | solution.py:128
  8.0 17.4 %collective-permute-start = (f32[1024]{0:T(1024)}, f32[1024]{0:T(1024)S(1)}, u32[]{:S(2)}, u32[]{:S(2)}) collective-permute-start(f32[1024]{0:T(1024)} %bitcast.66), channel_id=1, source_target_pairs={{0,8},{8,16},{16,24},{24,32},{32,40},{40,48},{48,56},{56,64},{64,7... | collective-permute-start | bytes 12296 | tf_op jit(solution)/shard_map/ppermute | solution.py:13
  26.0 6.1 %collective-permute-start.1 = (f32[1024]{0:T(1024)S(1)}, f32[1024]{0:T(1024)S(1)}, u32[]{:S(2)}, u32[]{:S(2)}) collective-permute-start(f32[1024]{0:T(1024)S(1)} %multiply_add_fusion.4), channel_id=1, source_target_pairs={{0,8},{8,16},{16,24},{24,32},{32,40},{40,48},{48,56},{56,64},{64,7... | collective-permute-start | bytes 12296 | tf_op jit(solution)/shard_map/ppermute | solution.py:13
  32.1 9.4 %collective-permute-start.2 = (f32[1024]{0:T(1024)S(1)}, f32[1024]{0:T(1024)S(1)}, u32[]{:S(2)}, u32[]{:S(2)}) collective-permute-start(f32[1024]{0:T(1024)S(1)} %multiply_add_fusion.3), channel_id=1, source_target_pairs={{0,8},{8,16},{16,24},{24,32},{32,40},{40,48},{48,56},{56,64},{64,7... | collective-permute-start | bytes 12296 | tf_op jit(solution)/shard_map/ppermute | solution.py:13
  42.2 19.6 %collective-permute-start.3 = (f32[1024]{0:T(1024)S(1)}, f32[1024]{0:T(1024)S(1)}, u32[]{:S(2)}, u32[]{:S(2)}) collective-permute-start(f32[1024]{0:T(1024)S(1)} %get-tuple-element.24), channel_id=1, source_target_pairs={{0,8},{8,16},{16,24},{24,32},{32,40},{40,48},{48,56},{56,64},{64,7... | collective-permute-start | bytes 12296 | tf_op jit(solution)/shard_map/ppermute | solution.py:13
  55.9 7.9 %copy-start.1 = (f32[1024,1024]{1,0:T(8,128)S(1)}, f32[1024,1024]{1,0:T(8,128)}, u32[]{:S(2)}) copy-start(f32[1024,1024]{1,0:T(8,128)} %fusion.12) | copy-start | bytes 12582916
  61.8 2.0 %copy-start.2 = (f32[1024,1024]{1,0:T(8,128)}, f32[1024,1024]{1,0:T(8,128)S(1)}, u32[]{:S(2)}) copy-start(f32[1024,1024]{1,0:T(8,128)S(1)} %get-tuple-element.45) | copy-start | bytes 12582916
  81.5 36.9 %copy-start.8 = (f32[1,3,1024]{2,0,1:T(1,128)S(1)}, f32[1,3,1024]{2,0,1:T(1,128)}, u32[]{:S(2)}) copy-start(f32[1,3,1024]{2,0,1:T(1,128)} %param.25) | copy-start | bytes 36868
  81.5 37.5 %copy-start.5 = (f32[1,16,1024]{2,1,0:T(8,128)S(1)}, f32[1,16,1024]{2,1,0:T(8,128)}, u32[]{:S(2)}) copy-start(f32[1,16,1024]{2,1,0:T(8,128)} %param.18) | copy-start | bytes 196612
  81.5 37.5 %copy-start.6 = (f32[1,16,1024]{2,1,0:T(8,128)S(1)}, f32[1,16,1024]{2,1,0:T(8,128)}, u32[]{:S(2)}) copy-start(f32[1,16,1024]{2,1,0:T(8,128)} %param.23) | copy-start | bytes 196612
  81.5 44.2 %copy-start.3 = (f32[1,128,1024]{2,1,0:T(8,128)S(1)}, f32[1,128,1024]{2,1,0:T(8,128)}, u32[]{:S(2)}) copy-start(f32[1,128,1024]{2,1,0:T(8,128)} %param.19) | copy-start | bytes 1572868
  81.5 44.2 %copy-start.4 = (f32[1,128,1024]{2,1,0:T(8,128)S(1)}, f32[1,128,1024]{2,1,0:T(8,128)}, u32[]{:S(2)}) copy-start(f32[1,128,1024]{2,1,0:T(8,128)} %param.24) | copy-start | bytes 1572868
Sparse Core Ops, SparseCore 0:
  10.1 45.7 all-gather.2
  69.2 56.5 reduce-scatter.1
where the time goes:
time: 137 us; the launch traced here: 136 us
  blocking collectives  33 us (24%)
  between operations  25.8 us (19%)
  starting transfers between devices  24.7 us (18%)
  matrix products  22.1 us (16%)
  waiting for transfers between devices  14.2 us (10%)
  other arithmetic  10.6 us (8%)
  local copies, waits for them, and re-layouts  5.35 us (4%)
    all_to_all x1, blocking collectives, copy_for_each(): lax.all_to_all(jnp.broadcast_to(value[None], (length, *value.shape)), axi...  33 us
    ppermute x4, starting transfers between devices, from_behind(): lax.ppermute(value, axis, [(source, source + steps) for source in range(l...  24.6 us
    all_gather x1, waiting for transfers between devices, full_rows(): return lax.all_gather(row_shard, 'path', axis=0, tiled=True)  7.46 us
    dot_general x1, matrix products, network_pass(): lax.dot_general(d_two_low, w_second, (((1,), (1,)), ((), ())), preferred_...  7.18 us
    reduce_scatter x1, waiting for transfers between devices, shards(): lax.psum_scatter(row_product(hidden_one, d_two_low).astype(jnp.bfloat16),...  6.04 us
    dot_general x1, matrix products, network_pass(): jnp.dot(hidden_one, w_second, preferred_element_type=jnp.float32)  5.9 us
    dot_general x1, matrix products, row_product(): lax.dot_general(hidden_one, d_two_low, (((0,), (0,)), ((), ())), preferre...  5.22 us
    reduce_sum x1, other arithmetic, network_pass(): d_bias_two = jnp.sum(d_pre_two, axis=0)  3.98 us
  transfers between devices with their start and end apart: 6, of which 2 were waited for; matrix products, arithmetic and copies ran while one was open for 21% of the time, Pallas kernels for 0%

commit v1 on v0

v1 whole, which is shorter than its diff:
```python
import jax
import jax.numpy as jnp
from jax import lax
from jax.experimental import pallas as pl
from jax.experimental.pallas import tpu as pltpu
from jax.sharding import PartitionSpec as P

MOMENTUM = 0.9
STEP_SIZE = 0.01
CHIPS = 4
HALVES = 2
F32 = jnp.float32
BF16 = jnp.bfloat16
ORDER = ((3, 2, 1, 0), (3, 0, 2, 1), (0, 3, 1, 2), (0, 1, 2, 3))


def from_behind(value, axis, steps):
    count = lax.axis_size(axis)
    return lax.ppermute(value, axis, [(source, source + steps) for source in range(count - steps)])


def sigmoid(u):
    return 0.5 * jnp.tanh(0.5 * u) + 0.5


def step_kernel(
    fac_ref,
    win_ref,
    vec_ref,
    shard_ref,
    gain_ref,
    rest_ref,
    mid_ref,
    small_ref,
    wfull,
    h1,
    h1t,
    slope,
    pre2,
    d2,
    grads,
    to_pair,
    from_pair,
    to_line,
    from_line,
    gain_col,
    small,
    small_pair,
    small_chip,
    small_sum,
    ag_send,
    ag_recv,
    pair_send,
    pair_recv,
    line_send,
    line_recv,
    small_send,
    small_recv,
    chip_send,
    chip_recv,
    sum_send,
    sum_recv,
):
    me = lax.axis_index("path")
    c = me // 2
    k = me % 2
    other = me + 1 - 2 * k
    hidden = h1.shape[1]
    paths = h1.shape[0]
    depth = shard_ref.shape[0]
    part = depth // HALVES
    half_columns = hidden // 2

    def remote(src, dst, send, recv, to):
        return pltpu.make_async_remote_copy(
            src_ref=src,
            dst_ref=dst,
            send_sem=send,
            recv_sem=recv,
            device_id={"path": to},
            device_id_type=pl.DeviceIdType.MESH,
        )

    barrier = pltpu.get_barrier_semaphore()
    pl.semaphore_signal(barrier, inc=1, device_id={"path": other}, device_id_type=pl.DeviceIdType.MESH)
    for far in range(1, CHIPS):
        pl.semaphore_signal(
            barrier,
            inc=1,
            device_id={"path": ((c + far) % CHIPS) * 2 + k},
            device_id_type=pl.DeviceIdType.MESH,
        )

    rows_first = 128
    gain_col[...] = jnp.transpose(jnp.broadcast_to(gain_ref[...], (8, paths)))

    def first_layer(m, carry):
        at = pl.ds(pl.multiple_of(m * rows_first, rows_first), rows_first)
        pre = (
            lax.dot_general(
                fac_ref[:, at], win_ref[...], (((0,), (0,)), ((), ())), preferred_element_type=F32
            )
            + vec_ref[0:1, :]
        )
        s = sigmoid(pre)
        act = pre * s
        slope[at, :] = s * (1.0 + pre * (1.0 - s))
        h1[at, :] = act.astype(BF16)
        h1t[:, at] = jnp.transpose(act).astype(BF16)
        return carry

    tiles_first = paths // rows_first
    lax.fori_loop(0, 1, first_layer, 0)
    pl.semaphore_wait(barrier, CHIPS)

    def rows_of(slot, h):
        return pl.ds(pl.multiple_of(slot * depth + h * part, part), part)

    LEFT, RIGHT, PAIR = 0, 1, 2

    def gather_copy(source, slot, h, way, to):
        return remote(
            source, wfull.at[rows_of(slot, h), :], ag_send.at[way, slot, h], ag_recv.at[slot, h], to
        )

    def shard_part(h):
        return shard_ref.at[pl.ds(h * part, part), :]

    for h in range(HALVES):

        @pl.when(c > 0)
        def _():
            gather_copy(shard_part(h), me, h, LEFT, me - 2).start()

        @pl.when(c < CHIPS - 1)
        def _():
            gather_copy(shard_part(h), me, h, RIGHT, me + 2).start()

    for h in range(HALVES):
        gather_copy(shard_part(h), me, h, PAIR, other).start()
    wfull[pl.ds(pl.multiple_of(me * depth, depth), depth), :] = shard_ref[...]
    lax.fori_loop(1, tiles_first, first_layer, 0)

    def landed(slot, h):
        at = wfull.at[rows_of(slot, h), :]
        gather_copy(at, slot, h, PAIR, other).wait_recv()

    def forward(slot, h, way, to):
        gather_copy(wfull.at[rows_of(slot, h), :], slot, h, way, to).start()

    def relay(far):
        for h in range(HALVES):

            @pl.when(c >= far)
            def _():
                slot = me - 2 * far
                landed(slot, h)

                @pl.when(c < CHIPS - 1)
                def _():
                    forward(slot, h, RIGHT, me + 2)

                forward(slot, h, PAIR, other)

            @pl.when(c + far < CHIPS)
            def _():
                slot = me + 2 * far
                landed(slot, h)

                @pl.when(c > 0)
                def _():
                    forward(slot, h, LEFT, me - 2)

                forward(slot, h, PAIR, other)

    tile = 256

    def middle(chip, first):
        columns = pl.ds(pl.multiple_of(chip * 2 * depth, 2 * depth), 2 * depth)

        def body(m, carry):
            at = pl.ds(pl.multiple_of(m * tile, tile), tile)
            product = jnp.dot(h1[at, columns], wfull[columns, :], preferred_element_type=F32)
            if first:
                pre2[at, :] = product + vec_ref[1:2, :]
            else:
                pre2[at, :] += product
            return carry

        lax.fori_loop(0, paths // tile, body, 0)

    def absorb(far):
        @pl.when(c >= far)
        def _():
            for h in range(HALVES):
                landed(other - 2 * far, h)
            middle(c - far, False)

        @pl.when(c + far < CHIPS)
        def _():
            for h in range(HALVES):
                landed(other + 2 * far, h)
            middle(c + far, False)

    relay(1)
    for h in range(HALVES):
        landed(other, h)
    middle(c, True)
    absorb(1)
    relay(2)
    absorb(2)
    relay(3)
    absorb(3)

    rows_second = 128

    def second_layer(m, carry):
        bias_two, head, value = carry
        at = pl.ds(pl.multiple_of(m * rows_second, rows_second), rows_second)
        pre = pre2[at, :]
        s = sigmoid(pre)
        act = (pre * s).astype(BF16).astype(F32)
        weights = vec_ref[2:3, :]
        chance = sigmoid(jnp.sum(act * weights, axis=1, keepdims=True))
        gain = gain_col[at, 0:1]
        d_logit = -gain * chance * (1.0 - chance)
        d_pre = d_logit * weights * (s * (1.0 + pre * (1.0 - s)))
        d2[at, :] = d_pre.astype(BF16)
        bias_two = bias_two + jnp.sum(d_pre, axis=0, keepdims=True)
        head = head + jnp.sum(d_logit * act, axis=0, keepdims=True)
        value = value + jnp.sum(chance * gain, axis=0, keepdims=True)
        return bias_two, head, value

    zero_row = jnp.zeros((1, hidden), F32)
    bias_two, head, value = lax.fori_loop(
        0, paths // rows_second, second_layer, (zero_row, zero_row, jnp.zeros((1, 1), F32))
    )
    small[17:18, :] = bias_two
    small[18:19, :] = head
    lane = lax.broadcasted_iota(jnp.int32, (1, hidden), 1)
    small[19:20, :] = rest_ref[...] + jnp.where(lane == 0, value, 0.0)
    small[20:24, :] = jnp.zeros((4, hidden), F32)

    def order(step):
        packed = sum(ORDER[chip][step] * 4**chip for chip in range(CHIPS))
        return lax.rem(lax.shift_right_logical(jnp.int32(packed), 2 * c), jnp.int32(4))

    def pair_copy(e):
        return remote(to_pair.at[e], from_pair.at[e], pair_send.at[e], pair_recv.at[e], other)

    def product(step):
        e = order(step)
        rows = pl.ds(pl.multiple_of(e * 2 * depth, 2 * depth), 2 * depth)

        def body(n, carry):
            at = pl.ds(pl.multiple_of(n * tile, tile), tile)
            grads[e, :, at] = jnp.dot(h1t[rows, :], d2[:, at], preferred_element_type=F32)
            return carry

        lax.fori_loop(0, hidden // tile, body, 0)
        theirs = pl.ds(pl.multiple_of((1 - k) * depth, depth), depth)
        to_pair[e] = grads[e, theirs, :].astype(BF16)
        pair_copy(e).start()

    def line_copy(way, e, h, to):
        at = pl.ds(h * part, part)
        return remote(
            to_line.at[e, at, :],
            from_line.at[way, e, at, :],
            line_send.at[e, h],
            line_recv.at[way, e, h],
            to,
        )

    def own_part(e, h):
        mine = pl.ds(pl.multiple_of(k * depth + h * part, part), part)
        return grads[e, mine, :] + from_pair[e, pl.ds(h * part, part), :].astype(F32)

    def along_line(step):
        e = order(step)
        pair_copy(e).wait_recv()
        for h in range(HALVES):
            at = pl.ds(h * part, part)

            @pl.when(e > c)
            def _():
                @pl.when(c == 0)
                def _():
                    to_line[e, at, :] = own_part(e, h).astype(BF16)

                @pl.when(c > 0)
                def _():
                    line_copy(0, e, h, other).wait_recv()
                    total = own_part(e, h) + from_line[0, e, at, :].astype(F32)
                    to_line[e, at, :] = total.astype(BF16)

                line_copy(0, e, h, me + 2).start()

            @pl.when(e < c)
            def _():
                @pl.when(c == CHIPS - 1)
                def _():
                    to_line[e, at, :] = own_part(e, h).astype(BF16)

                @pl.when(c < CHIPS - 1)
                def _():
                    line_copy(1, e, h, other).wait_recv()
                    total = own_part(e, h) + from_line[1, e, at, :].astype(F32)
                    to_line[e, at, :] = total.astype(BF16)

                line_copy(1, e, h, me - 2).start()

    at_end = c * (CHIPS - 1 - c) == 0
    product(0)
    product(1)
    pl.when(at_end)(lambda: along_line(0))
    product(2)
    pl.when(at_end)(lambda: along_line(1))
    product(3)
    pl.when(at_end)(lambda: along_line(2))

    def back(m, carry):
        bias_one, first = carry
        at = pl.ds(pl.multiple_of(m * tile, tile), tile)
        d_pre = (
            lax.dot_general(
                d2[at, :], wfull[...], (((1,), (1,)), ((), ())), preferred_element_type=F32
            )
            * slope[at, :]
        )
        bias_one = bias_one + jnp.sum(d_pre, axis=0, keepdims=True)
        first = first + jnp.dot(fac_ref[:, at], d_pre.astype(BF16), preferred_element_type=F32)
        return bias_one, first

    bias_one, first = lax.fori_loop(
        0, paths // tile, back, (zero_row, jnp.zeros((fac_ref.shape[0], hidden), F32))
    )
    small[0:16, :] = first
    small[16:17, :] = bias_one

    my_columns = pl.ds(pl.multiple_of(k * half_columns, half_columns), half_columns)
    their_columns = pl.ds(pl.multiple_of((1 - k) * half_columns, half_columns), half_columns)
    pair_sum = remote(small, small_pair, small_send, small_recv, other)
    pair_sum.start()
    pl.when(jnp.logical_not(at_end))(lambda: along_line(0))
    pair_sum.wait_recv()
    small_chip[c] = small[:, my_columns] + small_pair[:, my_columns]

    def chip_copy(far):
        to = ((c + far) % CHIPS) * 2 + k
        return remote(
            small_chip.at[c], small_chip.at[c], chip_send.at[far - 1], chip_recv.at[c], to
        )

    def chip_landed(far):
        chip = (c + far) % CHIPS
        slot = small_chip.at[chip]
        remote(slot, slot, chip_send.at[far - 1], chip_recv.at[chip], other).wait_recv()

    for far in range(1, CHIPS):
        chip_copy(far).start()
    pl.when(jnp.logical_not(at_end))(lambda: along_line(1))
    pl.when(jnp.logical_not(at_end))(lambda: along_line(2))
    for far in range(1, CHIPS):
        chip_landed(far)
    small_sum[:, my_columns] = small_chip[0] + small_chip[1] + small_chip[2] + small_chip[3]
    mine = small_sum.at[:, my_columns]
    theirs = small_sum.at[:, their_columns]
    share = remote(mine, mine, sum_send, sum_recv, other)
    share.start()

    pair_copy(c).wait_recv()
    for h in range(HALVES):
        mid_ref[pl.ds(h * part, part), :] = own_part(c, h)

    def arrived(way):
        for h in range(HALVES):
            at = pl.ds(h * part, part)
            line_copy(way, c, h, other).wait_recv()
            mid_ref[at, :] += from_line[way, c, at, :].astype(F32)

    pl.when(c > 0)(lambda: arrived(0))
    pl.when(c < CHIPS - 1)(lambda: arrived(1))
    remote(theirs, theirs, sum_send, sum_recv, other).wait_recv()
    small_ref[...] = small_sum[...]

    for h in range(HALVES):
        gather_copy(shard_part(h), me, h, PAIR, other).wait_send()

        @pl.when(c > 0)
        def _():
            gather_copy(shard_part(h), me, h, LEFT, me - 2).wait_send()

        @pl.when(c < CHIPS - 1)
        def _():
            gather_copy(shard_part(h), me, h, RIGHT, me + 2).wait_send()

        for far in range(1, CHIPS):

            @pl.when(c >= far)
            def _():
                slot = me - 2 * far
                source = wfull.at[rows_of(slot, h), :]
                gather_copy(source, slot, h, PAIR, other).wait_send()

                @pl.when(c < CHIPS - 1)
                def _():
                    gather_copy(source, slot, h, RIGHT, me + 2).wait_send()

            @pl.when(c + far < CHIPS)
            def _():
                slot = me + 2 * far
                source = wfull.at[rows_of(slot, h), :]
                gather_copy(source, slot, h, PAIR, other).wait_send()

                @pl.when(c > 0)
                def _():
                    gather_copy(source, slot, h, LEFT, me - 2).wait_send()

    for e in range(CHIPS):
        pair_copy(e).wait_send()
    for step in range(CHIPS - 1):
        for h in range(HALVES):
            line_copy(0, order(step), h, other).wait_send()
    pair_sum.wait_send()
    for far in range(1, CHIPS):
        chip_copy(far).wait_send()
    share.wait_send()


def run_step(factors, w_first, vectors, shard, gain_row, rest_row):
    paths = factors.shape[1]
    depth, hidden = shard.shape
    part_count = HALVES
    dma = pltpu.SemaphoreType.DMA
    vmem = pl.BlockSpec(memory_space=pltpu.VMEM)
    return pl.pallas_call(
        step_kernel,
        out_shape=(
            jax.ShapeDtypeStruct((depth, hidden), F32),
            jax.ShapeDtypeStruct((24, hidden), F32),
        ),
        in_specs=[vmem] * 6,
        out_specs=(vmem, vmem),
        scratch_shapes=[
            pltpu.VMEM((hidden, hidden), BF16),
            pltpu.VMEM((paths, hidden), BF16),
            pltpu.VMEM((hidden, paths), BF16),
            pltpu.VMEM((paths, hidden), F32),
            pltpu.VMEM((paths, hidden), F32),
            pltpu.VMEM((paths, hidden), BF16),
            pltpu.VMEM((CHIPS, 2 * depth, hidden), F32),
            pltpu.VMEM((CHIPS, depth, hidden), BF16),
            pltpu.VMEM((CHIPS, depth, hidden), BF16),
            pltpu.VMEM((CHIPS, depth, hidden), BF16),
            pltpu.VMEM((2, CHIPS, depth, hidden), BF16),
            pltpu.VMEM((paths, 8), F32),
            pltpu.VMEM((24, hidden), F32),
            pltpu.VMEM((24, hidden), F32),
            pltpu.VMEM((CHIPS, 24, hidden // 2), F32),
            pltpu.VMEM((24, hidden), F32),
            dma((3, 2 * CHIPS, part_count)),
            dma((2 * CHIPS, part_count)),
            dma((CHIPS,)),
            dma((CHIPS,)),
            dma((CHIPS, part_count)),
            dma((2, CHIPS, part_count)),
            dma,
            dma,
            dma((CHIPS - 1,)),
            dma((CHIPS,)),
            dma,
            dma,
        ],
        compiler_params=pltpu.CompilerParams(collective_id=0, has_side_effects=True),
        cost_estimate=pl.CostEstimate(
            flops=6 * paths * hidden * hidden, bytes_accessed=4 * hidden * hidden, transcendentals=0
        ),
    )(factors, w_first, vectors, shard, gain_row, rest_row)


def shards(
    factors,
    payoff,
    terminal,
    decisions,
    level_range,
    w_in_master,
    w_mid_master,
    vec_master,
    w_in_copy,
    w_mid_copy,
    mom_in,
    mom_mid,
    mom_vec,
):
    level_here = lax.axis_index("vol")
    dates = payoff.shape[0]
    paths_total = payoff.shape[1] * lax.axis_size("path")
    packed = jnp.concatenate([terminal, decisions[:, 0].astype(F32)], axis=0)
    below = [packed] + [from_behind(packed, "vol", back) for back in range(1, dates + 1)]
    carry = [rows[0] for rows in below]
    for date_index in range(dates - 1, 0, -1):
        lower_end = level_range[date_index, 0]
        upper_end = level_range[date_index, 1]
        after = []
        for j in range(len(carry) - 1):
            level = level_here - j
            inside = jnp.logical_and(level >= lower_end, level <= upper_end)
            taken = jnp.where(level > upper_end, 1.0, jnp.where(inside, below[j][date_index], 0.0))
            after.append(taken * (payoff[date_index] + carry[j + 1]) + (1.0 - taken) * carry[j])
        carry = after
    gain_row = payoff[0] + carry[1] - carry[0]
    low_now = level_range[0, 0]
    high_now = level_range[0, 1]
    active = jnp.logical_and(level_here >= low_now, level_here <= high_now)
    rest_row = jnp.where(level_here > high_now, gain_row, 0.0) + carry[0]
    gain_active = jnp.where(active, gain_row, 0.0)
    mid_grad, small = run_step(
        factors, w_in_copy[0], vec_master[0], w_mid_copy[0], gain_active[None], rest_row[None]
    )
    level_value = (jnp.sum(small[19]) / paths_total)[None]
    new_mom_in = MOMENTUM * mom_in + small[None, 0:16]
    new_mom_mid = MOMENTUM * mom_mid + mid_grad[None]
    new_mom_vec = MOMENTUM * mom_vec + small[None, 16:19]
    new_w_in = w_in_master - STEP_SIZE * new_mom_in
    new_w_mid = w_mid_master - STEP_SIZE * new_mom_mid
    new_vec = vec_master - STEP_SIZE * new_mom_vec
    return (
        level_value,
        new_w_in,
        new_w_mid,
        new_vec,
        new_mom_in,
        new_mom_mid,
        new_mom_vec,
        new_w_in.astype(BF16),
        new_w_mid.astype(BF16),
    )


def solution(mesh):
    in_specs = (
        P(None, "path"),
        P(None, "path"),
        P("vol", "path"),
        P(None, "vol", "path"),
        P(),
        P("vol", None, None),
        P("vol", "path", None),
        P("vol", None, None),
        P("vol", None, None),
        P("vol", "path", None),
        P("vol", None, None),
        P("vol", "path", None),
        P("vol", None, None),
    )
    out_specs = (
        P("vol"),
        P("vol", None, None),
        P("vol", "path", None),
        P("vol", None, None),
        P("vol", None, None),
        P("vol", "path", None),
        P("vol", None, None),
        P("vol", None, None),
        P("vol", "path", None),
    )
    return jax.shard_map(shards, mesh=mesh, in_specs=in_specs, out_specs=out_specs, check_vma=False)
```

time: 137 us -> 112 us (0.82)
  Pallas kernels: 0 us -> 58.4 us
  blocking collectives: 33 us -> 0 us
  matrix products: 22.1 us -> 0 us
  waiting for transfers between devices: 14.2 us -> 0.01 us
  starting transfers between devices: 24.7 us -> 20.1 us
  between operations: 25.8 us -> 22 us
  other arithmetic: 10.6 us -> 7.19 us
  local copies, waits for them, and re-layouts: 5.35 us -> 3.18 us
    pallas_call x0 -> x1, Pallas kernels: none -> 58.4 us  [run_step(): pl.pallas_call(step_kernel, out_shape=(jax.ShapeDtypeStruct((depth, hidde...]
    all_to_all x1 -> x0, blocking collectives: 33 us -> none  [copy_for_each(): lax.all_to_all(jnp.broadcast_to(value[None], (length, *value.shape)), axi...]
    dot_general x5 -> x0, matrix products: 22.1 us -> none  [the longest x1 7.18 us: network_pass(): lax.dot_general(d_two_low, w_second, (((1,), (1,)), ((), ())), preferred_...]
    all_gather x1 -> x0, waiting for transfers between devices: 7.46 us -> none  [full_rows(): return lax.all_gather(row_shard, 'path', axis=0, tiled=True)]
    reduce_scatter x1 -> x0, waiting for transfers between devices: 6.04 us -> none  [shards(): lax.psum_scatter(row_product(hidden_one, d_two_low).astype(jnp.bfloat16),...]
    ppermute x4, starting transfers between devices: 24.6 us -> 20.1 us  [from_behind(): lax.ppermute(value, axis, [(source, source + steps) for source in range(c...]
    reduce_sum x4 -> x1, other arithmetic: 5.66 us -> 1.44 us  [shards(): level_value = (jnp.sum(small[19]) / paths_total)[None]]
    slice x6 -> x1, local copies, waits for them, and re-layouts: 2.99 us -> 0.61 us  [shards(): low_now = level_range[0, 0]]
  transfers between devices with their start and end apart: 6 -> 4, of which waited for: 2 -> 0; matrix products, arithmetic and copies ran while one was open for 21% -> 1% of each run, Pallas kernels for 0% -> 0%
where the time goes in v1:
time: 112 us; the launch traced here: 111 us
  Pallas kernels  58.4 us (52%)
  between operations  22 us (20%)
  starting transfers between devices  20.1 us (18%)
  other arithmetic  7.19 us (6%)
  local copies, waits for them, and re-layouts  3.18 us (3%)
    pallas_call x1, Pallas kernels, run_step(): pl.pallas_call(step_kernel, out_shape=(jax.ShapeDtypeStruct((depth, hidde...  58.4 us
    ppermute x4, starting transfers between devices, from_behind(): lax.ppermute(value, axis, [(source, source + steps) for source in range(c...  20.1 us
    unnamed x23, local copies, waits for them, and re-layouts  2.58 us
  transfers between devices with their start and end apart: 4, of which 0 were waited for; matrix products, arithmetic and copies ran while one was open for 1% of the time, Pallas kernels for 0%

profile of v1, /device:TPU:1, one launch (start us, length us, event | category | flops | bytes accessed | tf_op | source)
XLA Modules:
  0.0 111.0 jit_solution(15008507623867972077)
XLA Ops:
  0.6 0.0 copy-start.7
  0.7 0.7 fusion.6
  1.4 0.0 copy-done.7
  1.4 0.0 copy-start.8
  1.4 8.3 %collective-permute-start = (f32[4,1024]{1,0:T(4,128)S(1)}, f32[4,1024]{1,0:T(4,128)S(1)}, u32[]{:S(2)}, u32[]{:S(2)}) collective-permute-start(f32[4,1024]{1,0:T(4,128)S(1)} %pad_maximum_fusion), channel_id=1, source_target_pairs={{0,8},{8,16},{16,24},{24,32},{32,40},{40,48},{48,56},{56,64},{64,7... | collective-permute-start | bytes 49160 | tf_op jit(solution)/shard_map/ppermute | solution.py:19
  9.7 3.1 %collective-permute-start.1 = (f32[4,1024]{1,0:T(4,128)S(1)}, f32[4,1024]{1,0:T(4,128)S(1)}, u32[]{:S(2)}, u32[]{:S(2)}) collective-permute-start(f32[4,1024]{1,0:T(4,128)S(1)} %pad_maximum_fusion), channel_id=1, source_target_pairs={{0,16},{8,24},{16,32},{24,40},{32,48},{40,56},{48,64},{56,72},{64,... | collective-permute-start | bytes 49160 | tf_op jit(solution)/shard_map/ppermute | solution.py:19
  12.8 3.3 %collective-permute-start.2 = (f32[4,1024]{1,0:T(4,128)S(1)}, f32[4,1024]{1,0:T(4,128)S(1)}, u32[]{:S(2)}, u32[]{:S(2)}) collective-permute-start(f32[4,1024]{1,0:T(4,128)S(1)} %pad_maximum_fusion), channel_id=1, source_target_pairs={{0,24},{8,32},{16,40},{24,48},{32,56},{40,64},{48,72},{56,80},{64,... | collective-permute-start | bytes 49160 | tf_op jit(solution)/shard_map/ppermute | solution.py:19
  16.1 5.4 %collective-permute-start.3 = (f32[4,1024]{1,0:T(4,128)S(1)}, f32[4,1024]{1,0:T(4,128)S(1)}, u32[]{:S(2)}, u32[]{:S(2)}) collective-permute-start(f32[4,1024]{1,0:T(4,128)S(1)} %pad_maximum_fusion), channel_id=1, source_target_pairs={{0,32},{8,40},{16,48},{24,56},{32,64},{40,72},{48,80},{56,88},{64,... | collective-permute-start | bytes 49160 | tf_op jit(solution)/shard_map/ppermute | solution.py:19
  21.6 0.0 copy-done.8
  21.6 0.6 fusion.9
  36.5 0.0 copy-start.6
  41.7 0.0 copy-done.6
  41.7 0.6 copy.37
  42.3 0.0 collective-permute-done
  42.3 0.0 collective-permute-done.1
  42.3 0.0 collective-permute-done.2
  42.3 0.7 copy-done.5
  43.0 0.1 multiply_add_fusion
  43.1 0.0 collective-permute-done.3
  43.1 0.7 fusion.3
  43.8 0.6 broadcast_select_fusion.19.gain_ref
  44.4 0.0 copy-start.1
  44.4 58.4 %shard_map.196 = (f32[128,1024]{1,0:T(8,128)}, f32[24,1024]{1,0:T(8,128)}) custom-call(bf16[16,1024]{1,0:T(8,128)(2,1)} %fac_ref.1, bf16[16,1024]{1,0:T(8,128)(2,1)} %bitcast.39, f32[3,1024]{1,0:T(4,128)} %bitcast.37, bf16[128,1024]{1,0:T(8,128)(2,1)} %bitcast.38, f32[1,1024]{1,0:T(1,128)} %broadcast_select_fusion.19.gain_ref, ...), custom_call_target="tpu_custom_call" | custom-call | flops 6442450944 | bytes 4194304 | tf_op jit(solution)/shard_map/pallas_call | solution.py:437
  102.8 1.4 %slice_reduce_fusion = f32[]{:T(128)} fusion(f32[24,1024]{1,0:T(8,128)} %get-tuple-element.11), kind=kLoop, calls=%fused_computation.37 | loop fusion | flops 1023 | bytes 4100 | tf_op jit(solution)/shard_map/reduce_sum | solution.py:522
  104.3 0.8 copy_subtract_fusion
  105.0 0.6 copy.25
  105.7 0.6 copy.26
  106.3 0.0 copy-done.4
  106.3 0.7 fusion.8
  107.6 0.0 copy-done
  107.6 0.0 copy-done.1
  107.6 2.2 %fusion.7 = (bf16[1,128,1024]{2,1,0:T(8,128)(2,1)}, f32[1,128,1024]{2,1,0:T(8,128)}, f32[1,128,1024]{2,1,0:T(8,128)}) fusion(f32[1,128,1024]{2,1,0:T(8,128)S(1)} %copy-done, f32[128,1024]{1,0:T(8,128)} %get-tuple-element.12, f32[1,128,1024]{2,1,0:T(8,128)S(1)} %copy-done.1), kind=kLoop, calls=%fused_computation.44 | loop fusion | flops 655360 | bytes 2883584 | tf_op jit(solution)/shard_map/convert_element_type | solution.py:538
  (10 shorter events, 0.0 us)
Async XLA Ops:
  0.6 0.7 copy-start.7
  1.4 20.2 %copy-start.8 = (s32[4,2]{0,1:T(2,128)S(1)}, s32[4,2]{0,1:T(2,128)}, u32[]{:S(2)}) copy-start(s32[4,2]{0,1:T(2,128)} %param.17) | copy-start | bytes 100
  1.4 40.9 %collective-permute-start = (f32[4,1024]{1,0:T(4,128)S(1)}, f32[4,1024]{1,0:T(4,128)S(1)}, u32[]{:S(2)}, u32[]{:S(2)}) collective-permute-start(f32[4,1024]{1,0:T(4,128)S(1)} %pad_maximum_fusion), channel_id=1, source_target_pairs={{0,8},{8,16},{16,24},{24,32},{32,40},{40,48},{48,56},{56,64},{64,7... | collective-permute-start | bytes 49160 | tf_op jit(solution)/shard_map/ppermute | solution.py:19
  9.7 32.6 %collective-permute-start.1 = (f32[4,1024]{1,0:T(4,128)S(1)}, f32[4,1024]{1,0:T(4,128)S(1)}, u32[]{:S(2)}, u32[]{:S(2)}) collective-permute-start(f32[4,1024]{1,0:T(4,128)S(1)} %pad_maximum_fusion), channel_id=1, source_target_pairs={{0,16},{8,24},{16,32},{24,40},{32,48},{40,56},{48,64},{56,72},{64,... | collective-permute-start | bytes 49160 | tf_op jit(solution)/shard_map/ppermute | solution.py:19
  12.8 29.5 %collective-permute-start.2 = (f32[4,1024]{1,0:T(4,128)S(1)}, f32[4,1024]{1,0:T(4,128)S(1)}, u32[]{:S(2)}, u32[]{:S(2)}) collective-permute-start(f32[4,1024]{1,0:T(4,128)S(1)} %pad_maximum_fusion), channel_id=1, source_target_pairs={{0,24},{8,32},{16,40},{24,48},{32,56},{40,64},{48,72},{56,80},{64,... | collective-permute-start | bytes 49160 | tf_op jit(solution)/shard_map/ppermute | solution.py:19
  16.1 27.0 %collective-permute-start.3 = (f32[4,1024]{1,0:T(4,128)S(1)}, f32[4,1024]{1,0:T(4,128)S(1)}, u32[]{:S(2)}, u32[]{:S(2)}) collective-permute-start(f32[4,1024]{1,0:T(4,128)S(1)} %pad_maximum_fusion), channel_id=1, source_target_pairs={{0,32},{8,40},{16,48},{24,56},{32,64},{40,72},{48,80},{56,88},{64,... | collective-permute-start | bytes 49160 | tf_op jit(solution)/shard_map/ppermute | solution.py:19
  36.5 5.2 %copy-start.6 = (f32[1,3,1024]{2,0,1:T(1,128)S(1)}, f32[1,3,1024]{2,0,1:T(1,128)}, u32[]{:S(2)}) copy-start(f32[1,3,1024]{2,0,1:T(1,128)} %param.20) | copy-start | bytes 36868
  42.3 0.7 copy-start.5
  44.4 59.9 %copy-start.9 = (f32[1,3,1024]{2,0,1:T(1,128)S(1)}, f32[1,3,1024]{2,0,1:T(1,128)}, u32[]{:S(2)}) copy-start(f32[1,3,1024]{2,0,1:T(1,128)} %param.25) | copy-start | bytes 36868
  44.4 61.9 %copy-start.3 = (f32[1,16,1024]{2,1,0:T(8,128)S(1)}, f32[1,16,1024]{2,1,0:T(8,128)}, u32[]{:S(2)}) copy-start(f32[1,16,1024]{2,1,0:T(8,128)} %param.18) | copy-start | bytes 196612
  44.4 61.9 %copy-start.4 = (f32[1,16,1024]{2,1,0:T(8,128)S(1)}, f32[1,16,1024]{2,1,0:T(8,128)}, u32[]{:S(2)}) copy-start(f32[1,16,1024]{2,1,0:T(8,128)} %param.23) | copy-start | bytes 196612
  44.4 63.2 %copy-start = (f32[1,128,1024]{2,1,0:T(8,128)S(1)}, f32[1,128,1024]{2,1,0:T(8,128)}, u32[]{:S(2)}) copy-start(f32[1,128,1024]{2,1,0:T(8,128)} %param.19) | copy-start | bytes 1572868
  44.4 63.2 %copy-start.1 = (f32[1,128,1024]{2,1,0:T(8,128)S(1)}, f32[1,128,1024]{2,1,0:T(8,128)}, u32[]{:S(2)}) copy-start(f32[1,128,1024]{2,1,0:T(8,128)} %param.24) | copy-start | bytes 1572868
  102.8 3.5 %copy-start.2 = (f32[24,1024]{1,0:T(8,128)S(1)}, f32[24,1024]{1,0:T(8,128)}, u32[]{:S(2)}) copy-start(f32[24,1024]{1,0:T(8,128)} %get-tuple-element.11) | copy-start | bytes 294916

commit v2 on v1

--- a/solution.py
+++ b/solution.py
@@ -1,3 +1,5 @@
+import functools
+
 import jax
 import jax.numpy as jnp
 from jax import lax
@@ -14,22 +16,19 @@
 ORDER = ((3, 2, 1, 0), (3, 0, 2, 1), (0, 3, 1, 2), (0, 1, 2, 3))
 
 
-def from_behind(value, axis, steps):
-    count = lax.axis_size(axis)
-    return lax.ppermute(value, axis, [(source, source + steps) for source in range(count - steps)])
-
-
 def sigmoid(u):
     return 0.5 * jnp.tanh(0.5 * u) + 0.5
 
 
 def step_kernel(
+    range_ref,
     fac_ref,
+    payoff_ref,
+    terminal_ref,
+    decisions_ref,
     win_ref,
     vec_ref,
     shard_ref,
-    gain_ref,
-    rest_ref,
     mid_ref,
     small_ref,
     wfull,
@@ -43,11 +42,15 @@
     from_pair,
     to_line,
     from_line,
+    level_out,
+    level_in,
     gain_col,
     small,
     small_pair,
     small_chip,
     small_sum,
+    level_send,
+    level_recv,
     ag_send,
     ag_recv,
     pair_send,
@@ -61,13 +64,16 @@
     sum_send,
     sum_recv,
 ):
+    level = lax.axis_index("vol")
+    levels = lax.axis_size("vol")
+    dates = payoff_ref.shape[0]
     me = lax.axis_index("path")
     c = me // 2
     k = me % 2
     other = me + 1 - 2 * k
     hidden = h1.shape[1]
     paths = h1.shape[0]
-    depth = shard_ref.shape[0]
+    depth = shard_ref.shape[1]
     part = depth // HALVES
     half_columns = hidden // 2
 
@@ -82,6 +88,11 @@
         )
 
     barrier = pltpu.get_barrier_semaphore()
+    for back in range(1, dates + 1):
+        for level_to in ((level + back) % levels, (level + levels - back) % levels):
+            pl.semaphore_signal(
+                barrier, inc=1, device_id={"vol": level_to}, device_id_type=pl.DeviceIdType.MESH
+            )
     pl.semaphore_signal(barrier, inc=1, device_id={"path": other}, device_id_type=pl.DeviceIdType.MESH)
     for far in range(1, CHIPS):
         pl.semaphore_signal(
@@ -91,16 +102,29 @@
             device_id_type=pl.DeviceIdType.MESH,
         )
 
+    level_out[0:1, :] = terminal_ref[...]
+    for date in range(1, dates):
+        level_out[date : date + 1, :] = decisions_ref[date - 1].astype(F32)
+
+    def level_copy(back):
+        return pltpu.make_async_remote_copy(
+            src_ref=level_out,
+            dst_ref=level_in.at[back - 1],
+            send_sem=level_send.at[back - 1],
+            recv_sem=level_recv.at[back - 1],
+            device_id={"vol": (level + back) % levels},
+            device_id_type=pl.DeviceIdType.MESH,
+        )
+
     rows_first = 128
-    gain_col[...] = jnp.transpose(jnp.broadcast_to(gain_ref[...], (8, paths)))
 
     def first_layer(m, carry):
         at = pl.ds(pl.multiple_of(m * rows_first, rows_first), rows_first)
         pre = (
             lax.dot_general(
-                fac_ref[:, at], win_ref[...], (((0,), (0,)), ((), ())), preferred_element_type=F32
+                fac_ref[:, at], win_ref[0], (((0,), (0,)), ((), ())), preferred_element_type=F32
             )
-            + vec_ref[0:1, :]
+            + vec_ref[0]
         )
         s = sigmoid(pre)
         act = pre * s
@@ -110,8 +134,9 @@
         return carry
 
     tiles_first = paths // rows_first
-    lax.fori_loop(0, 1, first_layer, 0)
-    pl.semaphore_wait(barrier, CHIPS)
+    tiles_ahead = tiles_first // 2
+    lax.fori_loop(0, tiles_ahead, first_layer, 0)
+    pl.semaphore_wait(barrier, CHIPS + 2 * dates)
 
     def rows_of(slot, h):
         return pl.ds(pl.multiple_of(slot * depth + h * part, part), part)
@@ -124,7 +149,7 @@
         )
 
     def shard_part(h):
-        return shard_ref.at[pl.ds(h * part, part), :]
+        return shard_ref.at[0, pl.ds(h * part, part), :]
 
     for h in range(HALVES):
 
@@ -138,8 +163,10 @@
 
     for h in range(HALVES):
         gather_copy(shard_part(h), me, h, PAIR, other).start()
-    wfull[pl.ds(pl.multiple_of(me * depth, depth), depth), :] = shard_ref[...]
-    lax.fori_loop(1, tiles_first, first_layer, 0)
+    wfull[pl.ds(pl.multiple_of(me * depth, depth), depth), :] = shard_ref[0]
+    for back in range(1, dates + 1):
+        level_copy(back).start()
+    lax.fori_loop(tiles_ahead, tiles_first, first_layer, 0)
 
     def landed(slot, h):
         at = wfull.at[rows_of(slot, h), :]
@@ -182,7 +209,7 @@
             at = pl.ds(pl.multiple_of(m * tile, tile), tile)
             product = jnp.dot(h1[at, columns], wfull[columns, :], preferred_element_type=F32)
             if first:
-                pre2[at, :] = product + vec_ref[1:2, :]
+                pre2[at, :] = product + vec_ref[1]
             else:
                 pre2[at, :] += product
             return carry
@@ -208,6 +235,33 @@
     middle(c, True)
     absorb(1)
     relay(2)
+
+    for back in range(1, dates + 1):
+        level_copy(back).wait_recv()
+
+    def of_level(back, row):
+        if back == 0:
+            return level_out[row : row + 1, :]
+        return jnp.where(level >= back, level_in[back - 1, row : row + 1, :], 0.0)
+
+    carry = [of_level(back, 0) for back in range(dates + 1)]
+    for date in range(dates - 1, 0, -1):
+        lower_end, upper_end = range_ref[0, date], range_ref[1, date]
+        after = []
+        for back in range(len(carry) - 1):
+            here = level - back
+            inside = jnp.logical_and(here >= lower_end, here <= upper_end)
+            free = jnp.where(inside, of_level(back, date), 0.0)
+            taken = jnp.where(here > upper_end, 1.0, free)
+            paid = payoff_ref[date : date + 1, :] + carry[back + 1]
+            after.append(taken * paid + (1.0 - taken) * carry[back])
+        carry = after
+    gain_row = payoff_ref[0:1, :] + carry[1] - carry[0]
+    active = jnp.logical_and(level >= range_ref[0, 0], level <= range_ref[1, 0])
+    rest_row = jnp.where(level > range_ref[1, 0], gain_row, 0.0) + carry[0]
+    gain_active = jnp.where(active, gain_row, 0.0)
+    gain_col[...] = jnp.transpose(jnp.broadcast_to(gain_active, (8, paths)))
+    small[19:20, :] = rest_row
     absorb(2)
     relay(3)
     absorb(3)
@@ -220,7 +274,7 @@
         pre = pre2[at, :]
         s = sigmoid(pre)
         act = (pre * s).astype(BF16).astype(F32)
-        weights = vec_ref[2:3, :]
+        weights = vec_ref[2]
         chance = sigmoid(jnp.sum(act * weights, axis=1, keepdims=True))
         gain = gain_col[at, 0:1]
         d_logit = -gain * chance * (1.0 - chance)
@@ -238,7 +292,7 @@
     small[17:18, :] = bias_two
     small[18:19, :] = head
     lane = lax.broadcasted_iota(jnp.int32, (1, hidden), 1)
-    small[19:20, :] = rest_ref[...] + jnp.where(lane == 0, value, 0.0)
+    small[19:20, :] += jnp.where(lane == 0, value, 0.0)
     small[20:24, :] = jnp.zeros((4, hidden), F32)
 
     def order(step):
@@ -276,10 +330,11 @@
         mine = pl.ds(pl.multiple_of(k * depth + h * part, part), part)
         return grads[e, mine, :] + from_pair[e, pl.ds(h * part, part), :].astype(F32)
 
-    def along_line(step):
+    def along_line(step, halves=range(HALVES)):
         e = order(step)
-        pair_copy(e).wait_recv()
-        for h in range(HALVES):
+        if 0 in halves:
+            pair_copy(e).wait_recv()
+        for h in halves:
             at = pl.ds(h * part, part)
 
             @pl.when(e > c)
@@ -332,9 +387,13 @@
         first = first + jnp.dot(fac_ref[:, at], d_pre.astype(BF16), preferred_element_type=F32)
         return bias_one, first
 
-    bias_one, first = lax.fori_loop(
-        0, paths // tile, back, (zero_row, jnp.zeros((fac_ref.shape[0], hidden), F32))
-    )
+    def on_the_way(step, h):
+        pl.when(jnp.logical_not(at_end))(lambda: along_line(step, (h,)))
+
+    sums = (zero_row, jnp.zeros((fac_ref.shape[0], hidden), F32))
+    sums = lax.fori_loop(0, paths // tile // 2, back, sums)
+    on_the_way(0, 0)
+    bias_one, first = lax.fori_loop(paths // tile // 2, paths // tile, back, sums)
     small[0:16, :] = first
     small[16:17, :] = bias_one
 
@@ -342,7 +401,7 @@
     their_columns = pl.ds(pl.multiple_of((1 - k) * half_columns, half_columns), half_columns)
     pair_sum = remote(small, small_pair, small_send, small_recv, other)
     pair_sum.start()
-    pl.when(jnp.logical_not(at_end))(lambda: along_line(0))
+    on_the_way(0, 1)
     pair_sum.wait_recv()
     small_chip[c] = small[:, my_columns] + small_pair[:, my_columns]
 
@@ -359,8 +418,9 @@
 
     for far in range(1, CHIPS):
         chip_copy(far).start()
-    pl.when(jnp.logical_not(at_end))(lambda: along_line(1))
-    pl.when(jnp.logical_not(at_end))(lambda: along_line(2))
+    for h in range(HALVES):
+        for step in (1, 2):
+            on_the_way(step, h)
     for far in range(1, CHIPS):
         chip_landed(far)
     small_sum[:, my_columns] = small_chip[0] + small_chip[1] + small_chip[2] + small_chip[3]
@@ -384,6 +444,8 @@
     remote(theirs, theirs, sum_send, sum_recv, other).wait_recv()
     small_ref[...] = small_sum[...]
 
+    for back in range(1, dates + 1):
+        level_copy(back).wait_send()
     for h in range(HALVES):
         gather_copy(shard_part(h), me, h, PAIR, other).wait_send()
 
@@ -428,9 +490,10 @@
     share.wait_send()
 
 
-def run_step(factors, w_first, vectors, shard, gain_row, rest_row):
+def run_step(level_range, factors, payoff, terminal, decisions, w_first, vectors, shard):
     paths = factors.shape[1]
-    depth, hidden = shard.shape
+    dates = payoff.shape[0]
+    _, depth, hidden = shard.shape
     part_count = HALVES
     dma = pltpu.SemaphoreType.DMA
     vmem = pl.BlockSpec(memory_space=pltpu.VMEM)
@@ -440,7 +503,7 @@
             jax.ShapeDtypeStruct((depth, hidden), F32),
             jax.ShapeDtypeStruct((24, hidden), F32),
         ),
-        in_specs=[vmem] * 6,
+        in_specs=[pl.BlockSpec(memory_space=pltpu.SMEM)] + [vmem] * 7,
         out_specs=(vmem, vmem),
         scratch_shapes=[
             pltpu.VMEM((hidden, hidden), BF16),
@@ -454,11 +517,15 @@
             pltpu.VMEM((CHIPS, depth, hidden), BF16),
             pltpu.VMEM((CHIPS, depth, hidden), BF16),
             pltpu.VMEM((2, CHIPS, depth, hidden), BF16),
+            pltpu.VMEM((8, paths), F32),
+            pltpu.VMEM((dates, 8, paths), F32),
             pltpu.VMEM((paths, 8), F32),
             pltpu.VMEM((24, hidden), F32),
             pltpu.VMEM((24, hidden), F32),
             pltpu.VMEM((CHIPS, 24, hidden // 2), F32),
             pltpu.VMEM((24, hidden), F32),
+            dma((dates,)),
+            dma((dates,)),
             dma((3, 2 * CHIPS, part_count)),
             dma((2 * CHIPS, part_count)),
             dma((CHIPS,)),
@@ -476,7 +543,61 @@
         cost_estimate=pl.CostEstimate(
             flops=6 * paths * hidden * hidden, bytes_accessed=4 * hidden * hidden, transcendentals=0
         ),
-    )(factors, w_first, vectors, shard, gain_row, rest_row)
+    )(level_range, factors, payoff, terminal, decisions, w_first, vectors, shard)
+
+
+def update_kernel(
+    mid_ref,
+    small_ref,
+    w_in_ref,
+    w_mid_ref,
+    vec_ref,
+    mom_in_ref,
+    mom_mid_ref,
+    mom_vec_ref,
+    value_ref,
+    new_w_in_ref,
+    new_w_mid_ref,
+    new_vec_ref,
+    new_mom_in_ref,
+    new_mom_mid_ref,
+    new_mom_vec_ref,
+    new_in_copy_ref,
+    new_mid_copy_ref,
+    *,
+    paths_total,
+):
+    value_ref[0] = jnp.sum(small_ref[19:20, :]) / paths_total
+
+    def update(grad, master, momentum, new_master, new_momentum, at):
+        moved = MOMENTUM * momentum[0, at, :] + grad
+        new_momentum[0, at, :] = moved
+        stepped = master[0, at, :] - STEP_SIZE * moved
+        new_master[0, at, :] = stepped
+        return stepped
+
+    factors = w_in_ref.shape[1]
+    everything = pl.ds(0, factors)
+    stepped = update(
+        small_ref[0:factors, :], w_in_ref, mom_in_ref, new_w_in_ref, new_mom_in_ref, everything
+    )
+    new_in_copy_ref[0] = stepped.astype(BF16)
+    for row in range(vec_ref.shape[0]):
+        at_row = small_ref[factors + row : factors + row + 1, :]
+        moved = MOMENTUM * mom_vec_ref[row] + at_row
+        new_mom_vec_ref[row] = moved
+        new_vec_ref[row] = vec_ref[row] - STEP_SIZE * moved
+    rows = 16
+
+    def body(i, carry):
+        at = pl.ds(pl.multiple_of(i * rows, rows), rows)
+        stepped = update(
+            mid_ref[at, :], w_mid_ref, mom_mid_ref, new_w_mid_ref, new_mom_mid_ref, at
+        )
+        new_mid_copy_ref[0, at, :] = stepped.astype(BF16)
+        return carry
+
+    lax.fori_loop(0, mid_ref.shape[0] // rows, body, 0)
 
 
 def shards(
@@ -494,49 +615,31 @@
     mom_mid,
     mom_vec,
 ):
-    level_here = lax.axis_index("vol")
-    dates = payoff.shape[0]
     paths_total = payoff.shape[1] * lax.axis_size("path")
-    packed = jnp.concatenate([terminal, decisions[:, 0].astype(F32)], axis=0)
-    below = [packed] + [from_behind(packed, "vol", back) for back in range(1, dates + 1)]
-    carry = [rows[0] for rows in below]
-    for date_index in range(dates - 1, 0, -1):
-        lower_end = level_range[date_index, 0]
-        upper_end = level_range[date_index, 1]
-        after = []
-        for j in range(len(carry) - 1):
-            level = level_here - j
-            inside = jnp.logical_and(level >= lower_end, level <= upper_end)
-            taken = jnp.where(level > upper_end, 1.0, jnp.where(inside, below[j][date_index], 0.0))
-            after.append(taken * (payoff[date_index] + carry[j + 1]) + (1.0 - taken) * carry[j])
-        carry = after
-    gain_row = payoff[0] + carry[1] - carry[0]
-    low_now = level_range[0, 0]
-    high_now = level_range[0, 1]
-    active = jnp.logical_and(level_here >= low_now, level_here <= high_now)
-    rest_row = jnp.where(level_here > high_now, gain_row, 0.0) + carry[0]
-    gain_active = jnp.where(active, gain_row, 0.0)
+    vectors = jnp.swapaxes(vec_master, 0, 1)
+    mom_rows = jnp.swapaxes(mom_vec, 0, 1)
     mid_grad, small = run_step(
-        factors, w_in_copy[0], vec_master[0], w_mid_copy[0], gain_active[None], rest_row[None]
+        level_range.T, factors, payoff, terminal, decisions, w_in_copy, vectors, w_mid_copy
     )
-    level_value = (jnp.sum(small[19]) / paths_total)[None]
-    new_mom_in = MOMENTUM * mom_in + small[None, 0:16]
-    new_mom_mid = MOMENTUM * mom_mid + mid_grad[None]
-    new_mom_vec = MOMENTUM * mom_vec + small[None, 16:19]
-    new_w_in = w_in_master - STEP_SIZE * new_mom_in
-    new_w_mid = w_mid_master - STEP_SIZE * new_mom_mid
-    new_vec = vec_master - STEP_SIZE * new_mom_vec
-    return (
-        level_value,
-        new_w_in,
-        new_w_mid,
-        new_vec,
-        new_mom_in,
-        new_mom_mid,
-        new_mom_vec,
-        new_w_in.astype(BF16),
-        new_w_mid.astype(BF16),
-    )
+    like = jax.ShapeDtypeStruct
+    vmem = pl.BlockSpec(memory_space=pltpu.VMEM)
+    outs = pl.pallas_call(
+        functools.partial(update_kernel, paths_total=paths_total),
+        out_shape=(
+            like((1,), F32),
+            like(w_in_master.shape, F32),
+            like(w_mid_master.shape, F32),
+            like(vectors.shape, F32),
+            like(w_in_master.shape, F32),
+            like(w_mid_master.shape, F32),
+            like(vectors.shape, F32),
+            like(w_in_master.shape, BF16),
+            like(w_mid_master.shape, BF16),
+        ),
+        in_specs=[vmem] * 8,
+        out_specs=(pl.BlockSpec(memory_space=pltpu.SMEM),) + (vmem,) * 8,
+    )(mid_grad, small, w_in_master, w_mid_master, vectors, mom_in, mom_mid, mom_rows)
+    return tuple(jnp.swapaxes(out, 0, 1) if at in (3, 6) else out for at, out in enumerate(outs))
 
 
 def solution(mesh):

time: 112 us -> 78 us (0.70)
  between operations: 22 us -> 0.65 us
  starting transfers between devices: 20.1 us -> 0 us
  Pallas kernels: 58.4 us -> 77.1 us
  other arithmetic: 7.19 us -> 0 us
  local copies, waits for them, and re-layouts: 3.18 us -> 0 us
    ppermute x4 -> x0, starting transfers between devices: 20.1 us -> none  [from_behind(): lax.ppermute(value, axis, [(source, source + steps) for source in range(c...]
    pallas_call x1, Pallas kernels: 58.4 us -> 74.2 us  [run_step(): pl.pallas_call(step_kernel, out_shape=(jax.ShapeDtypeStruct((depth, hidde...]
    convert_element_type x3 -> x0, other arithmetic: 3.63 us -> none  [the longest x1 2.24 us: shards(): new_w_mid.astype(BF16)]
    pallas_call x0 -> x1, Pallas kernels: none -> 2.9 us  [shards(): pl.pallas_call(functools.partial(update_kernel, paths_total=paths_total),...]
    unnamed x23 -> x0, local copies, waits for them, and re-layouts: 2.58 us -> none
    reduce_sum x1 -> x0, other arithmetic: 1.44 us -> none  [shards(): level_value = (jnp.sum(small[19]) / paths_total)[None]]
  transfers between devices with their start and end apart: 4 -> 0, of which waited for: 0 -> 0; matrix products, arithmetic and copies ran while one was open for 1% -> 0% of each run, Pallas kernels for 0% -> 0%
where the time goes in v2:
time: 78 us; the launch traced here: 77.8 us
  Pallas kernels  77.1 us (99%)
    pallas_call x1, Pallas kernels, run_step(): pl.pallas_call(step_kernel, out_shape=(jax.ShapeDtypeStruct((depth, hidde...  74.2 us
    pallas_call x1, Pallas kernels, shards(): pl.pallas_call(functools.partial(update_kernel, paths_total=paths_total),...  2.9 us

profile of v2, /device:TPU:1, one launch (start us, length us, event | category | flops | bytes accessed | tf_op | source)
XLA Modules:
  0.0 77.8 jit_solution(12443296110713986189)
XLA Ops:
  0.6 74.2 %shard_map.196 = (f32[128,1024]{1,0:T(8,128)}, f32[24,1024]{1,0:T(8,128)}) custom-call(s32[2,4]{1,0:T(2,128)} %bitcast.10, bf16[16,1024]{1,0:T(8,128)(2,1)} %fac_ref.1, f32[4,1024]{1,0:T(4,128)} %payoff_ref.1, f32[1,1024]{1,0:T(1,128)} %terminal_ref.1, s32[3,1,1024]{2,1,0:T(1,128)} %decisions_ref.1, bf16[1,16,1024]{2,1,0:T(8,128)(2,1)} %win_ref.1, ...), custom_call_target="tpu_custom_call" | custom-call | flops 6442450944 | bytes 4194304 | tf_op jit(solution)/shard_map/pallas_call | solution.py:500
  74.9 2.9 %shard_map.197 = (f32[1]{0:T(128)}, f32[1,16,1024]{2,1,0:T(8,128)}, f32[1,128,1024]{2,1,0:T(8,128)}, f32[3,1,1024]{2,1,0:T(1,128)}, f32[1,16,1024]{2,1,0:T(8,128...) custom-call(f32[128,1024]{1,0:T(8,128)} %get-tuple-element.20.mid_re, ...), custom_call_target="tpu_custom_call" | custom-call | tf_op jit(solution)/shard_map/pallas_call | solution.py:626

commit v3 on v2

--- a/solution.py
+++ b/solution.py
@@ -88,11 +88,18 @@
         )
 
     barrier = pltpu.get_barrier_semaphore()
-    for back in range(1, dates + 1):
-        for level_to in ((level + back) % levels, (level + levels - back) % levels):
-            pl.semaphore_signal(
-                barrier, inc=1, device_id={"vol": level_to}, device_id_type=pl.DeviceIdType.MESH
-            )
+
+    def greet_level(to):
+        pl.semaphore_signal(
+            barrier, inc=1, device_id={"vol": to}, device_id_type=pl.DeviceIdType.MESH
+        )
+
+    def each_level(above, below):
+        for back in range(1, dates + 1):
+            pl.when(level + back < levels)(functools.partial(above, back))
+            pl.when(level >= back)(functools.partial(below, back))
+
+    each_level(lambda back: greet_level(level + back), lambda back: greet_level(level - back))
     pl.semaphore_signal(barrier, inc=1, device_id={"path": other}, device_id_type=pl.DeviceIdType.MESH)
     for far in range(1, CHIPS):
         pl.semaphore_signal(
@@ -112,7 +119,7 @@
             dst_ref=level_in.at[back - 1],
             send_sem=level_send.at[back - 1],
             recv_sem=level_recv.at[back - 1],
-            device_id={"vol": (level + back) % levels},
+            device_id={"vol": level + back},
             device_id_type=pl.DeviceIdType.MESH,
         )
 
@@ -136,7 +143,10 @@
     tiles_first = paths // rows_first
     tiles_ahead = tiles_first // 2
     lax.fori_loop(0, tiles_ahead, first_layer, 0)
-    pl.semaphore_wait(barrier, CHIPS + 2 * dates)
+    peers = CHIPS
+    for back in range(1, dates + 1):
+        peers = peers + jnp.where(level + back < levels, 1, 0) + jnp.where(level >= back, 1, 0)
+    pl.semaphore_wait(barrier, peers)
 
     def rows_of(slot, h):
         return pl.ds(pl.multiple_of(slot * depth + h * part, part), part)
@@ -164,8 +174,13 @@
     for h in range(HALVES):
         gather_copy(shard_part(h), me, h, PAIR, other).start()
     wfull[pl.ds(pl.multiple_of(me * depth, depth), depth), :] = shard_ref[0]
+
+    def no_level(back):
+        level_in[back - 1] = jnp.zeros(level_in.shape[1:], F32)
+
     for back in range(1, dates + 1):
-        level_copy(back).start()
+        pl.when(level + back < levels)(level_copy(back).start)
+        pl.when(level < back)(functools.partial(no_level, back))
     lax.fori_loop(tiles_ahead, tiles_first, first_layer, 0)
 
     def landed(slot, h):
@@ -237,12 +252,12 @@
     relay(2)
 
     for back in range(1, dates + 1):
-        level_copy(back).wait_recv()
+        pl.when(level >= back)(level_copy(back).wait_recv)
 
     def of_level(back, row):
         if back == 0:
             return level_out[row : row + 1, :]
-        return jnp.where(level >= back, level_in[back - 1, row : row + 1, :], 0.0)
+        return level_in[back - 1, row : row + 1, :]
 
     carry = [of_level(back, 0) for back in range(dates + 1)]
     for date in range(dates - 1, 0, -1):
@@ -445,7 +460,7 @@
     small_ref[...] = small_sum[...]
 
     for back in range(1, dates + 1):
-        level_copy(back).wait_send()
+        pl.when(level + back < levels)(level_copy(back).wait_send)
     for h in range(HALVES):
         gather_copy(shard_part(h), me, h, PAIR, other).wait_send()
 

time: 78 us -> 68.7 us (0.88); the launches traced: 77.8 us -> 67.4 us
  Pallas kernels: 77.1 us -> 66.7 us
    pallas_call x1, Pallas kernels: 74.2 us -> 63.8 us  [run_step(): pl.pallas_call(step_kernel, out_shape=(jax.ShapeDtypeStruct((depth, hidde...]
where the time goes in v3:
time: 68.7 us; the launch traced here: 67.4 us
  Pallas kernels  66.7 us (97%)
    pallas_call x1, Pallas kernels, run_step(): pl.pallas_call(step_kernel, out_shape=(jax.ShapeDtypeStruct((depth, hidde...  63.8 us
    pallas_call x1, Pallas kernels, shards(): pl.pallas_call(functools.partial(update_kernel, paths_total=paths_total),...  2.9 us

profile of v3, /device:TPU:1, one launch (start us, length us, event | category | flops | bytes accessed | tf_op | source)
XLA Modules:
  0.0 67.4 jit_solution(15675660377982151137)
XLA Ops:
  0.6 63.8 %shard_map.196 = (f32[128,1024]{1,0:T(8,128)}, f32[24,1024]{1,0:T(8,128)}) custom-call(s32[2,4]{1,0:T(2,128)} %bitcast.10, bf16[16,1024]{1,0:T(8,128)(2,1)} %fac_ref.1, f32[4,1024]{1,0:T(4,128)} %payoff_ref.1, f32[1,1024]{1,0:T(1,128)} %terminal_ref.1, s32[3,1,1024]{2,1,0:T(1,128)} %decisions_ref.1, bf16[1,16,1024]{2,1,0:T(8,128)(2,1)} %win_ref.1, ...), custom_call_target="tpu_custom_call" | custom-call | flops 6442450944 | bytes 4194304 | tf_op jit(solution)/shard_map/pallas_call | solution.py:515
  64.5 2.9 %shard_map.197 = (f32[1]{0:T(128)}, f32[1,16,1024]{2,1,0:T(8,128)}, f32[1,128,1024]{2,1,0:T(8,128)}, f32[3,1,1024]{2,1,0:T(1,128)}, f32[1,16,1024]{2,1,0:T(8,128...) custom-call(f32[128,1024]{1,0:T(8,128)} %get-tuple-element.20.mid_re, ...), custom_call_target="tpu_custom_call" | custom-call | tf_op jit(solution)/shard_map/pallas_call | solution.py:641

commit v4 on v3

--- a/solution.py
+++ b/solution.py
@@ -22,6 +22,15 @@
 
 def step_kernel(
     range_ref,
+    fac_far,
+    payoff_far,
+    terminal_far,
+    decisions_far,
+    win_far,
+    vec_far,
+    shard_far,
+    mid_ref,
+    small_ref,
     fac_ref,
     payoff_ref,
     terminal_ref,
@@ -29,8 +38,7 @@
     win_ref,
     vec_ref,
     shard_ref,
-    mid_ref,
-    small_ref,
+    fetched,
     wfull,
     h1,
     h1t,
@@ -87,6 +95,22 @@
             device_id_type=pl.DeviceIdType.MESH,
         )
 
+    fetches = [
+        pltpu.make_async_copy(far, near, fetched.at[at])
+        for at, (far, near) in enumerate(
+            (
+                (terminal_far, terminal_ref),
+                (decisions_far, decisions_ref),
+                (fac_far, fac_ref),
+                (win_far, win_ref),
+                (vec_far, vec_ref),
+                (payoff_far, payoff_ref),
+                (shard_far, shard_ref),
+            )
+        )
+    ]
+    for fetch in fetches:
+        fetch.start()
     barrier = pltpu.get_barrier_semaphore()
 
     def greet_level(to):
@@ -109,6 +133,8 @@
             device_id_type=pl.DeviceIdType.MESH,
         )
 
+    for fetch in fetches:
+        fetch.wait()
     level_out[0:1, :] = terminal_ref[...]
     for date in range(1, dates):
         level_out[date : date + 1, :] = decisions_ref[date - 1].astype(F32)
@@ -135,7 +161,7 @@
         )
         s = sigmoid(pre)
         act = pre * s
-        slope[at, :] = s * (1.0 + pre * (1.0 - s))
+        slope[at, :] = s + act * (1.0 - s)
         h1[at, :] = act.astype(BF16)
         h1t[:, at] = jnp.transpose(act).astype(BF16)
         return carry
@@ -244,6 +270,7 @@
                 landed(other + 2 * far, h)
             middle(c + far, False)
 
+    at_end = c * (CHIPS - 1 - c) == 0
     relay(1)
     for h in range(HALVES):
         landed(other, h)
@@ -277,23 +304,29 @@
     gain_active = jnp.where(active, gain_row, 0.0)
     gain_col[...] = jnp.transpose(jnp.broadcast_to(gain_active, (8, paths)))
     small[19:20, :] = rest_row
-    absorb(2)
+    pl.when(at_end)(lambda: absorb(2))
     relay(3)
-    absorb(3)
+    last = (CHIPS - 1) * (1 - c // 2)
+    for h in range(HALVES):
+        landed(other + 2 * (last - c), h)
+    last_columns = pl.ds(pl.multiple_of(last * 2 * depth, 2 * depth), 2 * depth)
 
     rows_second = 128
 
     def second_layer(m, carry):
         bias_two, head, value = carry
         at = pl.ds(pl.multiple_of(m * rows_second, rows_second), rows_second)
-        pre = pre2[at, :]
+        pre = pre2[at, :] + jnp.dot(
+            h1[at, last_columns], wfull[last_columns, :], preferred_element_type=F32
+        )
         s = sigmoid(pre)
-        act = (pre * s).astype(BF16).astype(F32)
+        silu = pre * s
+        act = silu.astype(BF16).astype(F32)
         weights = vec_ref[2]
         chance = sigmoid(jnp.sum(act * weights, axis=1, keepdims=True))
         gain = gain_col[at, 0:1]
         d_logit = -gain * chance * (1.0 - chance)
-        d_pre = d_logit * weights * (s * (1.0 + pre * (1.0 - s)))
+        d_pre = d_logit * weights * (s + silu * (1.0 - s))
         d2[at, :] = d_pre.astype(BF16)
         bias_two = bias_two + jnp.sum(d_pre, axis=0, keepdims=True)
         head = head + jnp.sum(d_logit * act, axis=0, keepdims=True)
@@ -380,7 +413,6 @@
 
                 line_copy(1, e, h, me - 2).start()
 
-    at_end = c * (CHIPS - 1 - c) == 0
     product(0)
     product(1)
     pl.when(at_end)(lambda: along_line(0))
@@ -518,9 +550,15 @@
             jax.ShapeDtypeStruct((depth, hidden), F32),
             jax.ShapeDtypeStruct((24, hidden), F32),
         ),
-        in_specs=[pl.BlockSpec(memory_space=pltpu.SMEM)] + [vmem] * 7,
+        in_specs=[pl.BlockSpec(memory_space=pltpu.SMEM)]
+        + [pl.BlockSpec(memory_space=pltpu.HBM)] * 7,
         out_specs=(vmem, vmem),
         scratch_shapes=[
+            *(
+                pltpu.VMEM(a.shape, a.dtype)
+                for a in (factors, payoff, terminal, decisions, w_first, vectors, shard)
+            ),
+            dma((7,)),
             pltpu.VMEM((hidden, hidden), BF16),
             pltpu.VMEM((paths, hidden), BF16),
             pltpu.VMEM((hidden, paths), BF16),
@@ -554,7 +592,9 @@
             dma,
             dma,
         ],
-        compiler_params=pltpu.CompilerParams(collective_id=0, has_side_effects=True),
+        compiler_params=pltpu.CompilerParams(
+            collective_id=0, has_side_effects=True, vmem_limit_bytes=61 * 2**20
+        ),
         cost_estimate=pl.CostEstimate(
             flops=6 * paths * hidden * hidden, bytes_accessed=4 * hidden * hidden, transcendentals=0
         ),
@@ -653,6 +693,7 @@
         ),
         in_specs=[vmem] * 8,
         out_specs=(pl.BlockSpec(memory_space=pltpu.SMEM),) + (vmem,) * 8,
+        compiler_params=pltpu.CompilerParams(vmem_limit_bytes=8 * 2**20),
     )(mid_grad, small, w_in_master, w_mid_master, vectors, mom_in, mom_mid, mom_rows)
     return tuple(jnp.swapaxes(out, 0, 1) if at in (3, 6) else out for at, out in enumerate(outs))
 

time: 68.7 us -> 69.7 us (1.015)
  the two profiles are of different devices: /device:TPU:1 before, /device:TPU:199 now
where the time goes in v4:
time: 69.7 us; the launch traced here: 69.4 us
  Pallas kernels  66.7 us (96%)
  local copies, waits for them, and re-layouts  1.95 us (3%)
  between operations  0.76 us (1%)
    pallas_call x1, Pallas kernels, run_step(): pl.pallas_call(step_kernel, out_shape=(jax.ShapeDtypeStruct((depth, hidde...  65.3 us
    unnamed x16, local copies, waits for them, and re-layouts  1.95 us
    pallas_call x1, Pallas kernels, shards(): pl.pallas_call(functools.partial(update_kernel, paths_total=paths_total),...  1.4 us

profile of v4, /device:TPU:199, one launch (start us, length us, event | category | flops | bytes accessed | tf_op | source)
XLA Modules:
  0.0 69.4 jit_solution(16650837815449790505)
XLA Ops:
  0.6 0.0 copy-start
  0.7 0.0 copy-start.1
  0.7 0.0 copy-start.4
  0.7 0.0 copy-start.5
  0.7 0.0 copy-start.6
  0.7 0.0 copy-start.7
  0.7 65.3 %shard_map.196 = (f32[128,1024]{1,0:T(8,128)}, f32[24,1024]{1,0:T(8,128)}) custom-call(s32[2,4]{1,0:T(2,128)} %bitcast.10, bf16[16,1024]{1,0:T(8,128)(2,1)} %fac_far.1, f32[4,1024]{1,0:T(4,128)} %payoff_far.1, f32[1,1024]{1,0:T(1,128)} %terminal_far.1, s32[3,1,1024]{2,1,0:T(1,128)} %decisions_far.1, bf16[1,16,1024]{2,1,0:T(8,128)(2,1)} %win_far.1, ...), custom_call_target="tpu_custom_call" | custom-call | flops 6442450944 | bytes 4194304 | tf_op jit(solution)/shard_map/pallas_call | solution.py:547
  66.0 0.0 copy-done
  66.1 0.0 copy-done.1
  66.1 0.0 copy-done.4
  66.1 0.0 copy-done.5
  66.1 0.0 copy-done.6
  66.1 0.0 copy-done.7
  66.1 0.0 copy-start.2
  66.1 1.0 %copy-done.2 = f32[128,1024]{1,0:T(8,128)S(1)} copy-done((f32[128,1024]{1,0:T(8,128)S(1)}, f32[128,1024]{1,0:T(8,128)}, u32[]{:S(2)}) %copy-start.2) | copy-done | bytes 524312
  67.2 0.0 copy-start.3
  67.2 0.9 %copy-done.3 = f32[24,1024]{1,0:T(8,128)S(1)} copy-done((f32[24,1024]{1,0:T(8,128)S(1)}, f32[24,1024]{1,0:T(8,128)}, u32[]{:S(2)}) %copy-start.3) | copy-done | bytes 98328
  68.0 1.4 %shard_map.197 = (f32[1]{0:T(128)}, f32[1,16,1024]{2,1,0:T(8,128)}, f32[1,128,1024]{2,1,0:T(8,128)}, f32[3,1,1024]{2,1,0:T(1,128)}, f32[1,16,1024]{2,1,0:T(8,128...) custom-call(f32[128,1024]{1,0:T(8,128)S(1)} %copy-done.2, ...), custom_call_target="tpu_custom_call" | custom-call | tf_op jit(solution)/shard_map/pallas_call | solution.py:681
Async XLA Ops:
  0.6 65.4 %copy-start = (f32[1,128,1024]{2,1,0:T(8,128)S(1)}, f32[1,128,1024]{2,1,0:T(8,128)}, u32[]{:S(2)}) copy-start(f32[1,128,1024]{2,1,0:T(8,128)} %w_mid_ref.1) | copy-start | bytes 1572868
  0.7 65.4 %copy-start.1 = (f32[1,128,1024]{2,1,0:T(8,128)S(1)}, f32[1,128,1024]{2,1,0:T(8,128)}, u32[]{:S(2)}) copy-start(f32[1,128,1024]{2,1,0:T(8,128)} %mom_mid_ref.1) | copy-start | bytes 1572868
  0.7 65.4 %copy-start.4 = (f32[1,16,1024]{2,1,0:T(8,128)S(1)}, f32[1,16,1024]{2,1,0:T(8,128)}, u32[]{:S(2)}) copy-start(f32[1,16,1024]{2,1,0:T(8,128)} %w_in_ref.1) | copy-start | bytes 196612
  0.7 65.4 %copy-start.5 = (f32[1,16,1024]{2,1,0:T(8,128)S(1)}, f32[1,16,1024]{2,1,0:T(8,128)}, u32[]{:S(2)}) copy-start(f32[1,16,1024]{2,1,0:T(8,128)} %mom_in_ref.1) | copy-start | bytes 196612
  0.7 65.4 %copy-start.6 = (f32[1,3,1024]{2,0,1:T(1,128)S(1)}, f32[1,3,1024]{2,0,1:T(1,128)}, u32[]{:S(2)}) copy-start(f32[1,3,1024]{2,0,1:T(1,128)} %param.20) | copy-start | bytes 36868
  0.7 65.4 %copy-start.7 = (f32[1,3,1024]{2,0,1:T(1,128)S(1)}, f32[1,3,1024]{2,0,1:T(1,128)}, u32[]{:S(2)}) copy-start(f32[1,3,1024]{2,0,1:T(1,128)} %param.25) | copy-start | bytes 36868
  66.1 1.0 %copy-start.2 = (f32[128,1024]{1,0:T(8,128)S(1)}, f32[128,1024]{1,0:T(8,128)}, u32[]{:S(2)}) copy-start(f32[128,1024]{1,0:T(8,128)} %get-tuple-element.20.mid_ref) | copy-start | bytes 1572868
  67.2 0.9 %copy-start.3 = (f32[24,1024]{1,0:T(8,128)S(1)}, f32[24,1024]{1,0:T(8,128)}, u32[]{:S(2)}) copy-start(f32[24,1024]{1,0:T(8,128)} %get-tuple-element.21.small_ref) | copy-start | bytes 294916

commit v5 on v3

--- a/solution.py
+++ b/solution.py
@@ -135,7 +135,7 @@
         )
         s = sigmoid(pre)
         act = pre * s
-        slope[at, :] = s * (1.0 + pre * (1.0 - s))
+        slope[at, :] = s + act * (1.0 - s)
         h1[at, :] = act.astype(BF16)
         h1t[:, at] = jnp.transpose(act).astype(BF16)
         return carry
@@ -244,6 +244,7 @@
                 landed(other + 2 * far, h)
             middle(c + far, False)
 
+    at_end = c * (CHIPS - 1 - c) == 0
     relay(1)
     for h in range(HALVES):
         landed(other, h)
@@ -277,23 +278,29 @@
     gain_active = jnp.where(active, gain_row, 0.0)
     gain_col[...] = jnp.transpose(jnp.broadcast_to(gain_active, (8, paths)))
     small[19:20, :] = rest_row
-    absorb(2)
+    pl.when(at_end)(lambda: absorb(2))
     relay(3)
-    absorb(3)
+    last = (CHIPS - 1) * (1 - c // 2)
+    for h in range(HALVES):
+        landed(other + 2 * (last - c), h)
+    last_columns = pl.ds(pl.multiple_of(last * 2 * depth, 2 * depth), 2 * depth)
 
     rows_second = 128
 
     def second_layer(m, carry):
         bias_two, head, value = carry
         at = pl.ds(pl.multiple_of(m * rows_second, rows_second), rows_second)
-        pre = pre2[at, :]
+        pre = pre2[at, :] + jnp.dot(
+            h1[at, last_columns], wfull[last_columns, :], preferred_element_type=F32
+        )
         s = sigmoid(pre)
-        act = (pre * s).astype(BF16).astype(F32)
+        silu = pre * s
+        act = silu.astype(BF16).astype(F32)
         weights = vec_ref[2]
         chance = sigmoid(jnp.sum(act * weights, axis=1, keepdims=True))
         gain = gain_col[at, 0:1]
         d_logit = -gain * chance * (1.0 - chance)
-        d_pre = d_logit * weights * (s * (1.0 + pre * (1.0 - s)))
+        d_pre = d_logit * weights * (s + silu * (1.0 - s))
         d2[at, :] = d_pre.astype(BF16)
         bias_two = bias_two + jnp.sum(d_pre, axis=0, keepdims=True)
         head = head + jnp.sum(d_logit * act, axis=0, keepdims=True)
@@ -380,7 +387,6 @@
 
                 line_copy(1, e, h, me - 2).start()
 
-    at_end = c * (CHIPS - 1 - c) == 0
     product(0)
     product(1)
     pl.when(at_end)(lambda: along_line(0))
@@ -582,8 +588,6 @@
     *,
     paths_total,
 ):
-    value_ref[0] = jnp.sum(small_ref[19:20, :]) / paths_total
-
     def update(grad, master, momentum, new_master, new_momentum, at):
         moved = MOMENTUM * momentum[0, at, :] + grad
         new_momentum[0, at, :] = moved
@@ -591,17 +595,21 @@
         new_master[0, at, :] = stepped
         return stepped
 
-    factors = w_in_ref.shape[1]
-    everything = pl.ds(0, factors)
-    stepped = update(
-        small_ref[0:factors, :], w_in_ref, mom_in_ref, new_w_in_ref, new_mom_in_ref, everything
-    )
-    new_in_copy_ref[0] = stepped.astype(BF16)
-    for row in range(vec_ref.shape[0]):
-        at_row = small_ref[factors + row : factors + row + 1, :]
-        moved = MOMENTUM * mom_vec_ref[row] + at_row
-        new_mom_vec_ref[row] = moved
-        new_vec_ref[row] = vec_ref[row] - STEP_SIZE * moved
+    @pl.when(pl.program_id(0) == 0)
+    def _():
+        value_ref[0] = jnp.sum(small_ref[19:20, :]) / paths_total
+        factors = w_in_ref.shape[1]
+        everything = pl.ds(0, factors)
+        stepped = update(
+            small_ref[0:factors, :], w_in_ref, mom_in_ref, new_w_in_ref, new_mom_in_ref, everything
+        )
+        new_in_copy_ref[0] = stepped.astype(BF16)
+        for row in range(vec_ref.shape[0]):
+            at_row = small_ref[factors + row : factors + row + 1, :]
+            moved = MOMENTUM * mom_vec_ref[row] + at_row
+            new_mom_vec_ref[row] = moved
+            new_vec_ref[row] = vec_ref[row] - STEP_SIZE * moved
+
     rows = 16
 
     def body(i, carry):
@@ -637,7 +645,13 @@
         level_range.T, factors, payoff, terminal, decisions, w_in_copy, vectors, w_mid_copy
     )
     like = jax.ShapeDtypeStruct
-    vmem = pl.BlockSpec(memory_space=pltpu.VMEM)
+    steps = 4
+    depth, hidden = mid_grad.shape
+
+    def whole(array):
+        return pl.BlockSpec(array.shape, lambda i: (0,) * array.ndim)
+
+    block = pl.BlockSpec((1, depth // steps, hidden), lambda i: (0, i, 0))
     outs = pl.pallas_call(
         functools.partial(update_kernel, paths_total=paths_total),
         out_shape=(
@@ -651,8 +665,28 @@
             like(w_in_master.shape, BF16),
             like(w_mid_master.shape, BF16),
         ),
-        in_specs=[vmem] * 8,
-        out_specs=(pl.BlockSpec(memory_space=pltpu.SMEM),) + (vmem,) * 8,
+        grid=(steps,),
+        in_specs=[
+            pl.BlockSpec((depth // steps, hidden), lambda i: (i, 0)),
+            whole(small),
+            whole(w_in_master),
+            block,
+            whole(vectors),
+            whole(mom_in),
+            block,
+            whole(mom_rows),
+        ],
+        out_specs=(
+            pl.BlockSpec(memory_space=pltpu.SMEM),
+            whole(w_in_master),
+            block,
+            whole(vectors),
+            whole(w_in_master),
+            block,
+            whole(vectors),
+            whole(w_in_master),
+            block,
+        ),
     )(mid_grad, small, w_in_master, w_mid_master, vectors, mom_in, mom_mid, mom_rows)
     return tuple(jnp.swapaxes(out, 0, 1) if at in (3, 6) else out for at, out in enumerate(outs))
 

time: 68.7 us -> 70.4 us (1.025)
  Pallas kernels: 66.7 us -> 68.3 us
    pallas_call x1, Pallas kernels: 2.9 us -> 4.04 us  [shards(): pl.pallas_call(functools.partial(update_kernel, paths_total=paths_total),...]
where the time goes in v5:
time: 70.4 us; the launch traced here: 69 us
  Pallas kernels  68.3 us (97%)
    pallas_call x1, Pallas kernels, run_step(): pl.pallas_call(step_kernel, out_shape=(jax.ShapeDtypeStruct((depth, hidde...  64.3 us
    pallas_call x1, Pallas kernels, shards(): pl.pallas_call(functools.partial(update_kernel, paths_total=paths_total),...  4.04 us

profile of v5, /device:TPU:1, one launch (start us, length us, event | category | flops | bytes accessed | tf_op | source)
XLA Modules:
  0.0 69.0 jit_solution(17913924469670146895)
XLA Ops:
  0.6 64.3 %shard_map.196 = (f32[128,1024]{1,0:T(8,128)}, f32[24,1024]{1,0:T(8,128)}) custom-call(s32[2,4]{1,0:T(2,128)} %bitcast.10, bf16[16,1024]{1,0:T(8,128)(2,1)} %fac_ref.1, f32[4,1024]{1,0:T(4,128)} %payoff_ref.1, f32[1,1024]{1,0:T(1,128)} %terminal_ref.1, s32[3,1,1024]{2,1,0:T(1,128)} %decisions_ref.1, bf16[1,16,1024]{2,1,0:T(8,128)(2,1)} %win_ref.1, ...), custom_call_target="tpu_custom_call" | custom-call | flops 6442450944 | bytes 4194304 | tf_op jit(solution)/shard_map/pallas_call | solution.py:521
  64.9 4.0 %shard_map.197 = (f32[1]{0:T(128)}, f32[1,16,1024]{2,1,0:T(8,128)}, f32[1,128,1024]{2,1,0:T(8,128)}, f32[3,1,1024]{2,1,0:T(1,128)}, f32[1,16,1024]{2,1,0:T(8,128...) custom-call(f32[128,1024]{1,0:T(8,128)} %get-tuple-element.20.mid_re, ...), custom_call_target="tpu_custom_call" | custom-call | tf_op jit(solution)/shard_map/pallas_call | solution.py:655
